TPU v7x, 512 devices: a whole 4x8x8 slice. The times are simulated.
512 devices in a mesh: tile: 64 (over y, z), lev: 8 (over x, core).
Axes of the slice: x: 4, y: 8, z: 8, core: 2. Of those that a mesh axis runs over, the one named last changes fastest.
Arguments:
- adjoint: float32 [8, 256, 128, 128], P(None, 'tile', 'lev'), may hold values from -6 to 6
- courant: float32 [3, 256, 128, 128], P(None, 'tile', 'lev'), may hold values from -0.25 to 0.25
- diffusion: float32 [256, 128, 128], P('tile', 'lev'), may hold values from 0.01 to 0.06
- heights: int32 [256, 128], P('tile'), may hold values from 0 to 47, as said below
- dep_coef: float32 [8, 2097152], P(None, ('tile', 'lev')), may hold values from 0.02 to 0.2
- elem_dest: int32 [2097152, 1], P(('tile', 'lev')), may hold values from 0 to 63; in each aligned block of 4096 rows (0 to 4095, 4096 to 8191, ...) at most 128 rows name the same one
- elem_cell: int32 [2097152], P(('tile', 'lev')), may hold values from 0 to 8191
- seg_map: int32 [256, 128], P('tile'), may hold values from 0 to 4095, as said below
- emis_profile: float32 [128], P('lev'), may hold values from 0.004 to 0.04
Outputs:
- adjoint_old: float32 [8, 256, 128, 128], P(None, 'tile', 'lev')
- deposit_sense: float32 [8, 2097152], P(None, ('tile', 'lev'))
- segment_sense: float32 [8, 4096], P(None, ('tile', 'lev'))
Inputs may be any that keep to these rules, and one draw needn't show every extreme that they name: `elem_dest`: in the rows of one device at most 128 name the same tile, a bound that some block reaches of them. `heights`: constant over footprints of 4 x 4 columns; 0 in streets. `seg_map`: constant over patches of 4 x 8 columns.
All inputs are finite; a program needn't handle non-finite values.
Results may differ from a plain program's by a relative error of at most 0.00002.
Values sent between devices are 32-bit elements; how exact they have to be, the bound alone decides.
A program may use at most 64 MiB of HBM per device.

v0:
```python
import jax
import jax.numpy as jnp
from jax import lax
from jax.sharding import PartitionSpec as P

CAP = 128
SEG_DEV = 8


def padded_2(array, sides, width):
    for axis, dim in sides:
        count, length = (lax.axis_size(axis), array.shape[dim])
        up = [(i, (i + 1) % count) for i in range(count - 1)]
        down = [(j, i) for i, j in up]
        last = lax.slice_in_dim(array, length - width, length, axis=dim)
        first = lax.slice_in_dim(array, 0, width, axis=dim)
        before = lax.ppermute(last, axis, up)
        after = lax.ppermute(first, axis, down)
        array = jnp.concatenate([before, array, after], axis=dim)
    return array


def along_y(values, stride):
    zeroes = jnp.zeros_like(values[..., :1])
    if stride > 0:
        return jnp.concatenate([values[..., 1:], zeroes], axis=-1)
    return jnp.concatenate([zeroes, values[..., :-1]], axis=-1)


def interior(values):
    return values[..., 1:-1, 1:-1, :]


def offset_x(values, stride):
    extent = values.shape[-3]
    return values[..., 1 + stride : extent - 1 + stride, 1:-1, :]


def offset_z(values, stride):
    extent = values.shape[-2]
    return values[..., 1:-1, 1 + stride : extent - 1 + stride, :]


def face_terms(
    centre, forward, backward, diff_c, diff_f, diff_b, wet_c, wet_f, wet_b, cour_c, cour_b
):
    open_ahead = wet_c * wet_f
    open_behind = wet_b * wet_c
    cour_ahead = cour_c * open_ahead
    mix_ahead = 0.5 * (diff_c + diff_f) * open_ahead
    cour_behind = cour_b * open_behind
    mix_behind = 0.5 * (diff_b + diff_c) * open_behind
    return (jnp.maximum(cour_ahead, 0.0) + mix_ahead) * (forward - centre) + (
        jnp.minimum(cour_behind, 0.0) - mix_behind
    ) * (centre - backward)


def apply_adjoint(padded, diff_p, wet_p, cour_xp, cour_zp, cour_yc, deposit):
    centre = interior(padded)
    diff_c = interior(diff_p)
    wet_c = interior(wet_p)
    summed = face_terms(
        centre,
        offset_x(padded, 1),
        offset_x(padded, -1),
        diff_c,
        offset_x(diff_p, 1),
        offset_x(diff_p, -1),
        wet_c,
        offset_x(wet_p, 1),
        offset_x(wet_p, -1),
        interior(cour_xp),
        offset_x(cour_xp, -1),
    )
    summed = summed + face_terms(
        centre,
        offset_z(padded, 1),
        offset_z(padded, -1),
        diff_c,
        offset_z(diff_p, 1),
        offset_z(diff_p, -1),
        wet_c,
        offset_z(wet_p, 1),
        offset_z(wet_p, -1),
        interior(cour_zp),
        offset_z(cour_zp, -1),
    )
    summed = summed + face_terms(
        centre,
        along_y(centre, 1),
        along_y(centre, -1),
        diff_c,
        along_y(diff_c, 1),
        along_y(diff_c, -1),
        wet_c,
        along_y(wet_c, 1),
        along_y(wet_c, -1),
        cour_yc,
        along_y(cour_yc, -1),
    )
    return summed - deposit * centre


def local(
    adjoint, courant, diffusion, heights, dep_coef, elem_dest, elem_cell, seg_map, emis_profile
):
    tag_count, width_x, depth_z, width_y = adjoint.shape
    tile_count = lax.axis_size("tile")
    levels = lax.axis_index("lev") * depth_z + jnp.arange(depth_z, dtype=jnp.int32)
    wetness = (levels[None, :, None] >= heights[:, None, :]).astype(jnp.float32)
    dest_tile = elem_dest[:, 0]
    owners = jnp.arange(tile_count, dtype=jnp.int32)
    chosen = (dest_tile[:, None] == owners[None, :]).astype(jnp.int32)
    earlier = jnp.cumsum(chosen, axis=0) - chosen
    position = jnp.sum(earlier * chosen, axis=1)
    slot_index = dest_tile * CAP + position
    coef_buffer = (
        jnp.zeros((tag_count, tile_count * CAP), jnp.float32).at[:, slot_index].set(dep_coef)
    )
    cell_row = (
        jnp.full((tile_count * CAP,), -1.0, jnp.float32)
        .at[slot_index]
        .set(elem_cell.astype(jnp.float32))
    )
    outgoing = jnp.concatenate([coef_buffer, cell_row[None]], axis=0).reshape(
        tag_count + 1, tile_count, CAP
    )
    incoming = lax.all_to_all(outgoing, "tile", split_axis=1, concat_axis=1, tiled=True).reshape(
        tag_count + 1, tile_count * CAP
    )
    cell_ids = incoming[tag_count].astype(jnp.int32)
    filled = cell_ids >= 0
    safe_ids = jnp.where(filled, cell_ids, 0)
    arriving = incoming[:tag_count] * filled.astype(jnp.float32)[None]
    local_cells = width_x * depth_z * width_y
    deposit = (
        jax.ops.segment_sum(arriving.T, safe_ids, num_segments=local_cells).T.reshape(
            tag_count, width_x, depth_z, width_y
        )
        * wetness
    )
    flow_stack = jnp.stack([diffusion, wetness, courant[0], courant[2]])
    flow_p = padded_2(flow_stack, (("tile", 1), ("lev", 2)), 1)
    current = adjoint
    for divisor in (3.0, 2.0, 1.0):
        padded = padded_2(current, (("tile", 1), ("lev", 2)), 1)
        current = (
            adjoint
            + apply_adjoint(padded, flow_p[0], flow_p[1], flow_p[2], flow_p[3], courant[1], deposit)
            / divisor
        )
    flat_old = current.reshape(tag_count, -1)
    returning = (jnp.take(flat_old, safe_ids, axis=1) * arriving).reshape(
        tag_count, tile_count, CAP
    )
    returned = lax.all_to_all(returning, "tile", split_axis=1, concat_axis=1, tiled=True).reshape(
        tag_count, tile_count * CAP
    )
    deposit_sense = jnp.take(returned, slot_index, axis=1)
    weighting = wetness * emis_profile[None, :, None]
    columns = jnp.sum(current * weighting[None], axis=2).reshape(tag_count, -1)
    segment_total = SEG_DEV * tile_count * lax.axis_size("lev")
    partial_sums = jax.ops.segment_sum(columns.T, seg_map.reshape(-1), num_segments=segment_total).T
    segment_sense = lax.psum_scatter(partial_sums, ("tile", "lev"), scatter_dimension=1, tiled=True)
    return (current, deposit_sense, segment_sense)


def solution(mesh):
    placed = (
        P(None, "tile", "lev", None),
        P(None, "tile", "lev", None),
        P("tile", "lev", None),
        P("tile", None),
        P(None, ("tile", "lev")),
        P(("tile", "lev"), None),
        P(("tile", "lev")),
        P("tile", None),
        P("lev"),
    )
    return jax.shard_map(
        local,
        mesh=mesh,
        in_specs=placed,
        out_specs=(
            P(None, "tile", "lev", None),
            P(None, ("tile", "lev")),
            P(None, ("tile", "lev")),
        ),
        check_vma=False,
    )
```

profile of v0, /device:TPU:1, one launch (start us, length us, event | category | flops | bytes accessed | tf_op | source)
XLA Modules:
  0.0 572.7 jit_solution(5189320720043954062)
XLA Ops:
  7.2 0.8 slice_bitcast_fusion.4
  8.0 0.8 compare_convert_fusion.2
  8.7 0.7 pad_maximum_fusion.25
  9.5 4.8 collective-permute-start
  14.3 1.3 collective-permute-start.1
  15.6 0.9 fusion.9
  16.5 18.4 %reduce-window.6 = s32[64,32,128]{2,1,0:T(8,128)S(1)} reduce-window(s32[64,32,128]{2,1,0:T(8,128)S(1)} %fusion.9, s32[]{:T(128)} %constant.25.clone.1), window={size=1x1x128 pad=0_0x0_0x127_0}, to_apply=%region_0.0 | reduce-window | flops 33292288 | bytes 2097156 | tf_op jit(solution)/shard_map/reduce-window
  36.3 0.9 fusion.6
  37.9 12.8 %scatter_custom_fusion = f32[8,8192]{0,1:T(8,128)} fusion(s32[4096]{0:T(1024)S(1)} %bitcast.99, f32[4096,8]{1,0:T(8,128)S(1)} %copy.43, f32[]{:T(128)} %constant.22.clone.1), kind=kCustom, calls=%fused_computation.7 | custom fusion | bytes 262148 | tf_op jit(solution)/shard_map/scatter | solution.py:118
  50.7 2.8 copy.44
  53.5 15.5 %scatter_custom_fusion.1 = f32[8192]{0:T(1024)S(1)} fusion(s32[4096]{0:T(1024)S(1)} %bitcast.100, f32[4096]{0:T(1024)S(1)} %convert_element_type.68, f32[]{:T(128)} %constant.27.clone.1), kind=kCustom, calls=%fused_computation.149 | custom fusion | bytes 32772 | tf_op jit(solution)/shard_map/scatter | solution.py:123
  69.1 0.8 pad_maximum_fusion
  69.9 17.5 %all-to-all-start = ((f32[9,64,128]{2,0,1:T(8,128)}), f32[9,64,128]{2,0,1:T(8,128)S(1)}, u32[]{:S(2)}, u32[]{:S(2)}) async-start(f32[9,64,128]{2,0,1:T(8,128)} %pad_maximum_fusion), calls=%async_computation | async-start | bytes 1048576 | tf_op jit(solution)/shard_map/all_to_all | solution.py:128
  87.4 2.9 collective-permute-start.5
  90.3 1.3 collective-permute-start.4
  91.9 5.1 collective-permute-start.2
  97.0 1.9 collective-permute-start.3
  99.0 3.3 collective-permute-done.3
  102.5 0.8 fusion.61
  103.5 1.9 collective-permute-start.6
  105.5 3.6 collective-permute-start.7
  109.3 2.6 copy.47
  111.9 47.0 %scatter_custom_fusion.2 = f32[8192,8]{1,0:T(8,128)} fusion(s32[8192]{0:T(1024)S(1)} %bitcast.102, f32[8192,8]{1,0:T(8,128)} %copy.47, f32[]{:T(128)} %constant.22.clone.1), kind=kCustom, calls=%fused_computation.9 | custom fusion | flops 65536 | bytes 262656 | tf_op jit(solution)/shard_map/scatter-add | solution.py:137
  158.8 2.8 copy.48
  162.0 1.3 collective-permute-start.8
  163.3 6.3 %collective-permute-start.9 = (f32[8,1,16,128]{3,2,1,0:T(8,128)S(1)}, f32[8,1,16,128]{3,2,1,0:T(8,128)S(1)}, u32[]{:S(2)}, u32[]{:S(2)}) collective-permute-start(f32[8,1,16,128]{3,2,1,0:T(8,128)S(1)} %get-tuple-element.35), channel_id=1, source_target_pairs={{0,8},{8,16},{16,24},{24,32},{32,40},{40,48},{48,56},{56,64},{64,7... | collective-permute-start | bytes 196616 | tf_op jit(solution)/shard_map/ppermute | solution.py:17
  169.8 1.2 collective-permute-done.9
  171.0 1.9 collective-permute-start.10
  172.9 3.8 collective-permute-start.11
  176.8 0.7 collective-permute-done.11
  177.8 1.3 collective-permute-start.12
  179.1 6.9 %collective-permute-start.13 = (f32[8,1,16,128]{3,2,1,0:T(8,128)S(1)}, f32[8,1,16,128]{3,2,1,0:T(8,128)S(1)}, u32[]{:S(2)}, u32[]{:S(2)}) collective-permute-start(f32[8,1,16,128]{3,2,1,0:T(8,128)S(1)} %get-tuple-element.29), channel_id=1, source_target_pairs={{0,8},{8,16},{16,24},{24,32},{32,40},{40,48},{48,56},{56,64},{64,7... | collective-permute-start | bytes 196616 | tf_op jit(solution)/shard_map/ppermute | solution.py:17
  186.0 1.3 collective-permute-done.13
  187.4 1.9 collective-permute-start.14
  189.3 5.1 collective-permute-start.15
  194.5 0.8 collective-permute-done.15
  195.7 2.6 copy.49
  198.3 29.9 %gather_fusion = f32[8192,8]{1,0:T(8,128)} fusion(f32[8,8192]{0,1:T(8,128)} %bitcast.77, s32[8192]{0:T(1024)S(1)} %broadcast_clamp_fusion), kind=kCustom, calls=%fused_computation | custom fusion | bytes 557056 | tf_op jit(solution)/shard_map/jit(_take)/gather | solution.py:153
  228.2 2.8 copy.50
  231.0 0.8 multiply_multiply_fusion
  231.8 22.3 %all-to-all-start.1 = ((f32[8,64,128]{2,0,1:T(8,128)}), f32[8,64,128]{2,0,1:T(8,128)S(1)}, u32[]{:S(2)}, u32[]{:S(2)}) async-start(f32[8,64,128]{2,0,1:T(8,128)} %multiply_multiply_fusion), calls=%async_computation.1 | async-start | bytes 524288 | tf_op jit(solution)/shard_map/all_to_all | solution.py:156
  254.3 5.3 scatter_custom_fusion.3
  259.7 281.2 %all-reduce.14.cloned.1.call-done = f32[8,4096]{0,1:T(8,128)} async-done(((f32[8,4096]{0,1:T(8,128)}), f32[8,4096]{0,1:T(8,128)}) %all-reduce.14.cloned.1.call-update) | async-done | bytes 131088
  540.9 0.7 constant_dynamic-slice_fusion
  542.2 2.6 copy.51
  544.8 16.2 %gather_fusion.1 = f32[4096,8]{1,0:T(8,128)} fusion(f32[8,8192]{0,1:T(8,128)} %bitcast.79, s32[4096]{0:T(1024)S(1)} %broadcast_clamp_fusion.1), kind=kCustom, calls=%fused_computation.1 | custom fusion | bytes 278528 | tf_op jit(solution)/shard_map/jit(_take)/gather | solution.py:159
  561.1 3.6 select_bitcast_fusion
  564.7 1.2 copy.53
  (71 shorter events, 5.0 us)
Async XLA Ops:
  9.5 82.4 %collective-permute-start = (f32[4,1,16,128]{3,2,1,0:T(8,128)S(1)}, f32[4,1,16,128]{3,2,1,0:T(8,128)S(1)}, u32[]{:S(2)}, u32[]{:S(2)}) collective-permute-start(f32[4,1,16,128]{3,2,1,0:T(8,128)S(1)} %get-tuple-element.49), channel_id=1, source_target_pairs={{0,8},{8,16},{16,24},{24,32},{32,40},{40,48},{48,56},{56,64},{64,7... | collective-permute-start | bytes 98312 | tf_op jit(solution)/shard_map/ppermute | solution.py:17
  14.3 77.6 %collective-permute-start.1 = (f32[4,1,16,128]{3,2,1,0:T(8,128)S(1)}, f32[4,1,16,128]{3,2,1,0:T(8,128)S(1)}, u32[]{:S(2)}, u32[]{:S(2)}) collective-permute-start(f32[4,1,16,128]{3,2,1,0:T(8,128)S(1)} %get-tuple-element.50), channel_id=1, source_target_pairs={{8,0},{16,8},{24,16},{32,24},{40,32},{48,40},{56,48},{64,56},{72,6... | collective-permute-start | bytes 98312 | tf_op jit(solution)/shard_map/ppermute | solution.py:18
  15.6 20.7 %copy-start.3 = (s32[4096,1]{0,1:T(1,128)S(1)}, s32[4096,1]{0,1:T(1,128)}, u32[]{:S(2)}) copy-start(s32[4096,1]{0,1:T(1,128)} %param.14) | copy-start | bytes 49156
  16.5 20.8 %copy-start.4 = (f32[8,4096]{1,0:T(8,128)S(1)}, f32[8,4096]{1,0:T(8,128)}, u32[]{:S(2)}) copy-start(f32[8,4096]{1,0:T(8,128)} %param.13) | copy-start | bytes 393220
  37.9 15.6 %copy-start.6 = (s32[4096]{0:T(1024)S(1)}, s32[4096]{0:T(1024)}, u32[]{:S(2)}) copy-start(s32[4096]{0:T(1024)} %param.15) | copy-start | bytes 49156
  50.7 36.7 %copy-start = (f32[8,4,16,128]{3,2,1,0:T(8,128)S(1)}, f32[8,4,16,128]{3,2,1,0:T(8,128)}, u32[]{:S(2)}) copy-start(f32[8,4,16,128]{3,2,1,0:T(8,128)} %param.9) | copy-start | bytes 786436
  50.7 41.1 %copy-start.5 = (s32[4,128]{1,0:T(4,128)S(1)}, s32[4,128]{1,0:T(4,128)}, u32[]{:S(2)}) copy-start(s32[4,128]{1,0:T(4,128)} %param.12) | copy-start | bytes 6148
  50.7 41.1 %copy-start.7 = (f32[16]{0:T(128)S(1)}, f32[16]{0:T(128)}, u32[]{:S(2)}) copy-start(f32[16]{0:T(128)} %param.17) | copy-start | bytes 196
  50.7 41.2 %copy-start.2 = (f32[4,16,128]{2,1,0:T(8,128)S(1)}, f32[4,16,128]{2,1,0:T(8,128)}, u32[]{:S(2)}) copy-start(f32[4,16,128]{2,1,0:T(8,128)} %param.11) | copy-start | bytes 98308
  69.9 39.2 %all-to-all-start = ((f32[9,64,128]{2,0,1:T(8,128)}), f32[9,64,128]{2,0,1:T(8,128)S(1)}, u32[]{:S(2)}, u32[]{:S(2)}) async-start(f32[9,64,128]{2,0,1:T(8,128)} %pad_maximum_fusion), calls=%async_computation | async-start | bytes 1048576 | tf_op jit(solution)/shard_map/all_to_all | solution.py:128
  87.4 16.0 %collective-permute-start.5 = (f32[8,1,16,128]{3,2,1,0:T(8,128)S(1)}, f32[8,1,16,128]{3,2,1,0:T(8,128)S(1)}, u32[]{:S(2)}, u32[]{:S(2)}) collective-permute-start(f32[8,1,16,128]{3,2,1,0:T(8,128)S(1)} %get-tuple-element.40), channel_id=1, source_target_pairs={{0,8},{8,16},{16,24},{24,32},{32,40},{40,48},{48,56},{56,64},{64,7... | collective-permute-start | bytes 196616 | tf_op jit(solution)/shard_map/ppermute | solution.py:17
  90.3 13.1 %collective-permute-start.4 = (f32[8,1,16,128]{3,2,1,0:T(8,128)S(1)}, f32[8,1,16,128]{3,2,1,0:T(8,128)S(1)}, u32[]{:S(2)}, u32[]{:S(2)}) collective-permute-start(f32[8,1,16,128]{3,2,1,0:T(8,128)S(1)} %get-tuple-element.39), channel_id=1, source_target_pairs={{8,0},{16,8},{24,16},{32,24},{40,32},{48,40},{56,48},{64,56},{72,6... | collective-permute-start | bytes 196616 | tf_op jit(solution)/shard_map/ppermute | solution.py:18
  91.9 7.1 %collective-permute-start.2 = (f32[4,6,1,128]{3,2,1,0:T(1,128)S(1)}, f32[4,6,1,128]{3,2,1,0:T(1,128)S(1)}, u32[]{:S(2)}, u32[]{:S(2)}) collective-permute-start(f32[4,6,1,128]{3,2,1,0:T(1,128)S(1)} %get-tuple-element.45), channel_id=1, source_target_pairs={{0,1},{1,2},{2,3},{3,4},{4,5},{5,6},{6,7},{8,9},{9,10},{10,11},{11... | collective-permute-start | bytes 36872 | tf_op jit(solution)/shard_map/ppermute | solution.py:17
  97.0 5.3 collective-permute-start.3
  103.5 58.1 %collective-permute-start.6 = (f32[8,6,1,128]{3,2,1,0:T(1,128)S(1)}, f32[8,6,1,128]{3,2,1,0:T(1,128)S(1)}, u32[]{:S(2)}, u32[]{:S(2)}) collective-permute-start(f32[8,6,1,128]{3,2,1,0:T(1,128)S(1)} %get-tuple-element.23), channel_id=1, source_target_pairs={{1,0},{2,1},{3,2},{4,3},{5,4},{6,5},{7,6},{9,8},{10,9},{11,10},{12... | collective-permute-start | bytes 73736 | tf_op jit(solution)/shard_map/ppermute | solution.py:18
  105.5 56.2 %collective-permute-start.7 = (f32[8,6,1,128]{3,2,1,0:T(1,128)S(1)}, f32[8,6,1,128]{3,2,1,0:T(1,128)S(1)}, u32[]{:S(2)}, u32[]{:S(2)}) collective-permute-start(f32[8,6,1,128]{3,2,1,0:T(1,128)S(1)} %get-tuple-element.24), channel_id=1, source_target_pairs={{0,1},{1,2},{2,3},{3,4},{4,5},{5,6},{6,7},{8,9},{9,10},{10,11},{11... | collective-permute-start | bytes 73736 | tf_op jit(solution)/shard_map/ppermute | solution.py:17
  162.0 7.8 %collective-permute-start.8 = (f32[8,1,16,128]{3,2,1,0:T(8,128)S(1)}, f32[8,1,16,128]{3,2,1,0:T(8,128)S(1)}, u32[]{:S(2)}, u32[]{:S(2)}) collective-permute-start(f32[8,1,16,128]{3,2,1,0:T(8,128)S(1)} %get-tuple-element.36), channel_id=1, source_target_pairs={{8,0},{16,8},{24,16},{32,24},{40,32},{48,40},{56,48},{64,56},{72,6... | collective-permute-start | bytes 196616 | tf_op jit(solution)/shard_map/ppermute | solution.py:18
  163.3 7.6 %collective-permute-start.9 = (f32[8,1,16,128]{3,2,1,0:T(8,128)S(1)}, f32[8,1,16,128]{3,2,1,0:T(8,128)S(1)}, u32[]{:S(2)}, u32[]{:S(2)}) collective-permute-start(f32[8,1,16,128]{3,2,1,0:T(8,128)S(1)} %get-tuple-element.35), channel_id=1, source_target_pairs={{0,8},{8,16},{16,24},{24,32},{32,40},{40,48},{48,56},{56,64},{64,7... | collective-permute-start | bytes 196616 | tf_op jit(solution)/shard_map/ppermute | solution.py:17
  171.0 5.8 %collective-permute-start.10 = (f32[8,6,1,128]{3,2,1,0:T(1,128)S(1)}, f32[8,6,1,128]{3,2,1,0:T(1,128)S(1)}, u32[]{:S(2)}, u32[]{:S(2)}) collective-permute-start(f32[8,6,1,128]{3,2,1,0:T(1,128)S(1)} %get-tuple-element.21), channel_id=1, source_target_pairs={{1,0},{2,1},{3,2},{4,3},{5,4},{6,5},{7,6},{9,8},{10,9},{11,10},{12... | collective-permute-start | bytes 73736 | tf_op jit(solution)/shard_map/ppermute | solution.py:18
  172.9 4.6 collective-permute-start.11
  177.8 8.2 %collective-permute-start.12 = (f32[8,1,16,128]{3,2,1,0:T(8,128)S(1)}, f32[8,1,16,128]{3,2,1,0:T(8,128)S(1)}, u32[]{:S(2)}, u32[]{:S(2)}) collective-permute-start(f32[8,1,16,128]{3,2,1,0:T(8,128)S(1)} %get-tuple-element.30), channel_id=1, source_target_pairs={{8,0},{16,8},{24,16},{32,24},{40,32},{48,40},{56,48},{64,56},{72,6... | collective-permute-start | bytes 196616 | tf_op jit(solution)/shard_map/ppermute | solution.py:18
  179.1 8.2 %collective-permute-start.13 = (f32[8,1,16,128]{3,2,1,0:T(8,128)S(1)}, f32[8,1,16,128]{3,2,1,0:T(8,128)S(1)}, u32[]{:S(2)}, u32[]{:S(2)}) collective-permute-start(f32[8,1,16,128]{3,2,1,0:T(8,128)S(1)} %get-tuple-element.29), channel_id=1, source_target_pairs={{0,8},{8,16},{16,24},{24,32},{32,40},{40,48},{48,56},{56,64},{64,7... | collective-permute-start | bytes 196616 | tf_op jit(solution)/shard_map/ppermute | solution.py:17
  187.4 7.1 %collective-permute-start.14 = (f32[8,6,1,128]{3,2,1,0:T(1,128)S(1)}, f32[8,6,1,128]{3,2,1,0:T(1,128)S(1)}, u32[]{:S(2)}, u32[]{:S(2)}) collective-permute-start(f32[8,6,1,128]{3,2,1,0:T(1,128)S(1)} %get-tuple-element.19), channel_id=1, source_target_pairs={{1,0},{2,1},{3,2},{4,3},{5,4},{6,5},{7,6},{9,8},{10,9},{11,10},{12... | collective-permute-start | bytes 73736 | tf_op jit(solution)/shard_map/ppermute | solution.py:18
  189.3 6.0 %collective-permute-start.15 = (f32[8,6,1,128]{3,2,1,0:T(1,128)S(1)}, f32[8,6,1,128]{3,2,1,0:T(1,128)S(1)}, u32[]{:S(2)}, u32[]{:S(2)}) collective-permute-start(f32[8,6,1,128]{3,2,1,0:T(1,128)S(1)} %get-tuple-element.20), channel_id=1, source_target_pairs={{0,1},{1,2},{2,3},{3,4},{4,5},{5,6},{6,7},{8,9},{9,10},{10,11},{11... | collective-permute-start | bytes 73736 | tf_op jit(solution)/shard_map/ppermute | solution.py:17
  195.7 35.3 %copy-start.1 = (f32[8,4,16,128]{3,2,1,0:T(8,128)}, f32[8,4,16,128]{3,2,1,0:T(8,128)S(1)}, u32[]{:S(2)}) copy-start(f32[8,4,16,128]{3,2,1,0:T(8,128)S(1)} %get-tuple-element.16) | copy-start | bytes 786436
  231.8 310.5 %all-to-all-start.1 = ((f32[8,64,128]{2,0,1:T(8,128)}), f32[8,64,128]{2,0,1:T(8,128)S(1)}, u32[]{:S(2)}, u32[]{:S(2)}) async-start(f32[8,64,128]{2,0,1:T(8,128)} %multiply_multiply_fusion), calls=%async_computation.1 | async-start | bytes 524288 | tf_op jit(solution)/shard_map/all_to_all | solution.py:156
  254.1 286.8 %all-reduce.14.cloned.1.call-start = ((), (), s32[]{:S(2)}) async-start(), calls=%async_computation.2 | async-start | bytes 4194304
Sparse Core Ops, SparseCore 0:
  259.9 280.9 all-reduce.13
where the time goes:
time: 574 us; the launch traced here: 573 us
  waiting for transfers between devices  289 us (50%)
  local copies, waits for them, and re-layouts  96.2 us (17%)
  starting transfers between devices  91.3 us (16%)
  other arithmetic  82.1 us (14%)
  between operations  14.6 us (3%)
    unnamed x2, waiting for transfers between devices  281 us
    scatter-add x1, other arithmetic, local(): jax.ops.segment_sum(arriving.T, safe_ids, num_segments=local_cells)  47 us
    ppermute x8, starting transfers between devices, padded_2(): before = lax.ppermute(last, axis, up)  38.6 us
    gather x2, local copies, waits for them, and re-layouts, local(): jnp.take(flat_old, safe_ids, axis=1) * arriving  32.7 us
    all_to_all x1, starting transfers between devices, local(): lax.all_to_all(returning, 'tile', split_axis=1, concat_axis=1, tiled=True)  22.3 us
    another operation x3, other arithmetic  19 us
    all_to_all x1, starting transfers between devices, local(): lax.all_to_all(outgoing, 'tile', split_axis=1, concat_axis=1, tiled=True)  17.5 us
    gather x1, local copies, waits for them, and re-layouts, local(): deposit_sense = jnp.take(returned, slot_index, axis=1)  16.2 us
  transfers between devices with their start and end apart: 19, of which 6 were waited for; matrix products, arithmetic and copies ran while one was open for 20% of the time, Pallas kernels for 0%

commit v1 on v0

v1 whole, which is shorter than its diff:
```python
import functools

import jax
import jax.numpy as jnp
from jax import lax
from jax.experimental import pallas as pl
from jax.experimental.pallas import tpu as pltpu
from jax.sharding import PartitionSpec as P

MESH = pl.DeviceIdType.MESH
LANES = 128
F32 = jnp.float32
BF16 = jnp.bfloat16
I32 = jnp.int32
HIGHEST = lax.Precision.HIGHEST


def split2(values):
    first = values.astype(BF16)
    return first, (values - first.astype(F32)).astype(BF16)


def iota(shape, dim):
    return lax.broadcasted_iota(I32, shape, dim)


def rows_to(row, count):
    return jnp.broadcast_to(row, (count, row.shape[-1]))


def nt_dot(a, b, precision=None):
    return lax.dot_general(
        a, b, (((1,), (1,)), ((), ())), precision=precision, preferred_element_type=F32
    )


def one_hot_256(row_int):
    local = rows_to(row_int, 16) - iota((16, row_int.shape[-1]), 0)
    local = local.astype(F32).astype(BF16)
    one, zero = jnp.ones((), BF16), jnp.zeros((), BF16)
    return [jnp.where(local == jnp.full((), 16 * j, BF16), one, zero) for j in range(16)]


def step_kernel(
    n_tile,
    n_lev,
    adj,
    cour,
    diff,
    hts,
    coef,
    dest,
    cell,
    seg,
    emis,
    old_out,
    sense_out,
    seg_out,
    state,
    dep,
    weights,
    wet_s,
    zpad,
    fx_r,
    fx_l,
    fz_u,
    fz_d,
    one_d,
    pref,
    pack_a,
    pack_b,
    snd,
    rcv,
    dep_a,
    cell_b,
    cell_hi,
    dest_hi,
    acc,
    look,
    snd2,
    rcv2,
    look2,
    rows,
    s_a2a,
    r_a2a,
    s_back,
    r_back,
    s_flow,
    r_flow,
    s_halo,
    r_halo,
    s_row,
    r_row,
):
    me = lax.axis_index("tile")
    lev = lax.axis_index("lev")
    right, left = lax.rem(me + 1, n_tile), lax.rem(me + n_tile - 1, n_tile)
    above, below = lax.rem(lev + 1, n_lev), lax.rem(lev + n_lev - 1, n_lev)
    tags, elements = coef.shape
    chunks = elements // LANES
    half = n_tile // 2
    depth = 16
    width = 4

    barrier = pltpu.get_barrier_semaphore()

    def greet(k, carry):
        pl.semaphore_signal(
            barrier,
            inc=1,
            device_id=(lax.rem(me + k, n_tile), lev),
            device_id_type=MESH,
        )
        return carry

    lax.fori_loop(1, n_tile, greet, 0)
    for j in range(1, n_lev):
        pl.semaphore_signal(
            barrier, inc=1, device_id=(me, lax.rem(lev + j, n_lev)), device_id_type=MESH
        )

    def reorder(z, carry):
        for x in range(width):
            state[0, x + 1, z + 1] = adj[pl.ds(x * depth + z, tags, stride=width * depth), :]
        return carry

    lax.fori_loop(0, depth, reorder, 0)

    levels = iota((depth, LANES), 0) + lev * depth
    for x in range(width):
        wet_s[x] = (levels >= rows_to(hts[x : x + 1, :], depth)).astype(F32)
    fx_r[0, 0] = wet_s[width - 1]
    fx_r[0, 1] = diff[width - 1]
    fx_r[0, 2] = cour[0, width - 1]
    fx_l[0, 0] = wet_s[0]
    fx_l[0, 1] = diff[0]
    for x in range(width):
        fz_u[0, x : x + 1] = diff[x, depth - 1 : depth, :]
        fz_u[0, width + x : width + x + 1] = cour[2, x, depth - 1 : depth, :]
        fz_d[0, x : x + 1] = diff[x, 0:1, :]
        fz_d[0, width + x : width + x + 1] = cour[2, x, 0:1, :]

    def mark(c, carry):
        k_row = (dest[pl.ds(c, 1), :] - me + n_tile) & (n_tile - 1)
        one_d[pl.ds(pl.multiple_of(c * n_tile, n_tile), n_tile), :] = (
            (rows_to(k_row, n_tile) == iota((n_tile, LANES), 0)).astype(F32).astype(BF16)
        )
        return carry

    lax.fori_loop(0, chunks, mark, 0)
    upper = (iota((LANES, 2 * LANES), 0) < iota((LANES, 2 * LANES), 1)).astype(F32).astype(BF16)
    pref[...] = jnp.dot(one_d[...], upper, preferred_element_type=F32)

    sub_half = iota((16, LANES), 0) // 8

    def place(c, before):
        at = pl.ds(pl.multiple_of(c * LANES, LANES), LANES)
        k_row = (dest[pl.ds(c, 1), :] - me + n_tile) & (n_tile - 1)
        block = pl.ds(pl.multiple_of(c * n_tile, n_tile), n_tile)
        mine = rows_to(k_row, n_tile) == iota((n_tile, LANES), 0)
        place_row = jnp.sum(
            jnp.where(mine, pref[block, 0:LANES] + before, 0.0), axis=0, keepdims=True
        ).astype(I32)
        hi_row = k_row & (half - 1)
        lo_row = (k_row // half) * LANES + place_row
        dest_hi[pl.ds(c, 1), :] = hi_row
        for j, piece in enumerate(one_hot_256(lo_row)):
            pack_b[16 * j : 16 * j + 16, at] = piece
        first, second = split2(coef[:, at])
        first = jnp.concatenate([first, first], axis=0)
        second = jnp.concatenate([second, second], axis=0)
        local = (rows_to(hi_row, 16) - sub_half).astype(F32).astype(BF16)
        zero = jnp.zeros((), BF16)
        for j in range(half // 2):
            chosen = local == jnp.full((), 2 * j, BF16)
            pack_a[16 * j : 16 * j + 16, at] = jnp.where(chosen, first, zero)
            pack_a[half * 8 + 16 * j : half * 8 + 16 * j + 16, at] = jnp.where(
                chosen, second, zero
            )
        id_row = cell[pl.ds(c, 1), :].astype(F32)
        id_all = jnp.where(
            rows_to(hi_row, half) == iota((half, LANES), 0), rows_to(id_row, half), 0.0
        )
        id_first, id_second = split2(id_all)
        pack_a[half * 16 : half * 17, at] = id_first
        pack_a[half * 17 : half * 18, at] = id_second
        return before + pref[block, LANES : 2 * LANES]

    lax.fori_loop(0, chunks, place, jnp.zeros((n_tile, LANES), F32))
    packed = nt_dot(pack_a[...], pack_b[...])
    for k in range(n_tile):
        hi, lo = k % half, (k // half) * LANES
        snd[k, 0:tags, :] = (
            packed[hi * 8 : hi * 8 + 8, lo : lo + LANES]
            + packed[half * 8 + hi * 8 : half * 8 + hi * 8 + 8, lo : lo + LANES]
        )
        snd[k, tags : tags + 1, :] = (
            packed[half * 16 + hi : half * 16 + hi + 1, lo : lo + LANES]
            + packed[half * 17 + hi : half * 17 + hi + 1, lo : lo + LANES]
        )
        snd[k, tags + 1 : tags + 2, :] = seg[0:1, :].astype(F32)

    pl.semaphore_wait(barrier, n_tile - 1 + n_lev - 1)

    def forward(k):
        return pltpu.make_async_remote_copy(
            src_ref=snd.at[k],
            dst_ref=rcv.at[k],
            send_sem=s_a2a.at[k],
            recv_sem=r_a2a.at[k],
            device_id=(lax.rem(me + k, n_tile), lev),
            device_id_type=MESH,
        )

    def back(k):
        return pltpu.make_async_remote_copy(
            src_ref=snd2.at[k],
            dst_ref=rcv2.at[k],
            send_sem=s_back.at[k],
            recv_sem=r_back.at[k],
            device_id=(lax.rem(me + n_tile - k, n_tile), lev),
            device_id_type=MESH,
        )

    def start_forward(k, carry):
        forward(k).start()
        return carry

    lax.fori_loop(1, n_tile, start_forward, 0)
    rcv[0] = snd[0]

    def halos(step):
        return [
            pltpu.make_async_remote_copy(
                src_ref=source,
                dst_ref=target,
                send_sem=s_halo.at[step, i],
                recv_sem=r_halo.at[step, i],
                device_id=device,
                device_id_type=MESH,
            )
            for i, (source, target, device) in enumerate(
                (
                    (
                        state.at[step, width, pl.ds(1, depth)],
                        state.at[step, 0, pl.ds(1, depth)],
                        (right, lev),
                    ),
                    (
                        state.at[step, 1, pl.ds(1, depth)],
                        state.at[step, width + 1, pl.ds(1, depth)],
                        (left, lev),
                    ),
                    (
                        state.at[step, pl.ds(1, width), depth],
                        state.at[step, pl.ds(1, width), 0],
                        (me, above),
                    ),
                    (
                        state.at[step, pl.ds(1, width), 1],
                        state.at[step, pl.ds(1, width), depth + 1],
                        (me, below),
                    ),
                )
            )
        ]

    flows = [
        pltpu.make_async_remote_copy(
            src_ref=ref.at[0],
            dst_ref=ref.at[1],
            send_sem=s_flow.at[i],
            recv_sem=r_flow.at[i],
            device_id=device,
            device_id_type=MESH,
        )
        for i, (ref, device) in enumerate(
            ((fx_r, (right, lev)), (fx_l, (left, lev)), (fz_u, (me, above)), (fz_d, (me, below)))
        )
    ]
    for copy in flows:
        copy.start()
    for copy in halos(0):
        copy.start()

    for copy in flows:
        copy.wait_recv()
    inner_left = (me > 0).astype(F32)
    inner_right = (me < n_tile - 1).astype(F32)
    wet_p = [fx_r[1, 0] * inner_left] + [wet_s[x] for x in range(width)] + [fx_l[1, 0] * inner_right]
    diff_p = [fx_r[1, 1]] + [diff[x] for x in range(width)] + [fx_l[1, 1]]
    cour_p = [fx_r[1, 2]] + [cour[0, x] for x in range(width)]

    def face(wet_a, wet_b, diff_a, diff_b, courant):
        opened = wet_a * wet_b
        a = courant * opened
        k = 0.5 * (diff_a + diff_b) * opened
        return jnp.maximum(a, 0.0) + k, k - jnp.minimum(a, 0.0)

    for f in range(width + 1):
        ahead, behind = face(wet_p[f], wet_p[f + 1], diff_p[f], diff_p[f + 1], cour_p[f])
        if f > 0:
            weights[0, f - 1] = ahead
        if f < width:
            weights[1, f] = behind
    last_lane = iota((depth, LANES), 1) == LANES - 1
    for x in range(width):
        zpad[0, 8 : 8 + depth] = diff[x]
        zpad[0, 7:8] = fz_u[1, x : x + 1]
        zpad[0, 8 + depth : 9 + depth] = fz_d[1, x : x + 1]
        zpad[1, 8 : 8 + depth] = cour[2, x]
        zpad[1, 7:8] = fz_u[1, width + x : width + x + 1]
        height = rows_to(hts[x : x + 1, :], depth)
        wet = wet_s[x]
        wet_up = ((levels + 1 >= height) & (levels + 1 < n_lev * depth)).astype(F32)
        wet_dn = ((levels - 1 >= height) & (levels >= 1)).astype(F32)
        ahead, _ = face(wet, wet_up, diff[x], zpad[0, 9 : 9 + depth], cour[2, x])
        _, behind = face(wet_dn, wet, zpad[0, 7 : 7 + depth], diff[x], zpad[1, 7 : 7 + depth])
        weights[2, x] = ahead
        weights[3, x] = behind
        wet_next = jnp.where(last_lane, 0.0, pltpu.roll(wet, LANES - 1, 1))
        ahead, behind = face(wet, wet_next, diff[x], pltpu.roll(diff[x], LANES - 1, 1), cour[1, x])
        weights[4, x] = ahead
        weights[5, x] = pltpu.roll(behind, 1, 1)

    group = dep_a.shape[1] // LANES
    acc[...] = jnp.zeros_like(acc)

    def gather_group(g, carry):
        for i in range(group):
            k = g * group + i

            @pl.when(k > 0)
            def _():
                forward(k).wait_recv()

            at = pl.ds(pl.multiple_of(k * LANES, LANES), LANES)
            id_row = rcv[k, tags : tags + 1, :].astype(I32)
            hi_row = ((id_row >> 11) & 1) * 16 + ((id_row >> 7) & 15)
            lo_row = (id_row >> 12) * LANES + (id_row & 127)
            cell_hi[pl.ds(k, 1), :] = hi_row
            for j, piece in enumerate(one_hot_256(lo_row)):
                cell_b[16 * j : 16 * j + 16, at] = piece
            first, second = split2(rcv[k, 0:tags, :])
            first = jnp.concatenate([first, first], axis=0)
            second = jnp.concatenate([second, second], axis=0)
            local = (rows_to(hi_row, 16) - sub_half).astype(F32).astype(BF16)
            zero = jnp.zeros((), BF16)
            for j in range(16):
                chosen = local == jnp.full((), 2 * j, BF16)
                dep_a[16 * j : 16 * j + 16, i * LANES : (i + 1) * LANES] = jnp.where(
                    chosen, first, zero
                )
                dep_a[256 + 16 * j : 272 + 16 * j, i * LANES : (i + 1) * LANES] = jnp.where(
                    chosen, second, zero
                )
        span = pl.ds(pl.multiple_of(g * group * LANES, group * LANES), group * LANES)
        acc[...] += nt_dot(dep_a[...], cell_b[:, span])
        return carry

    lax.fori_loop(0, n_tile // group, gather_group, 0)

    def finish_deposit(z, carry):
        for x in range(width):
            row = pl.multiple_of(((x & 1) * depth + z) * 8, 8)
            lo = (x >> 1) * LANES
            total = acc[pl.ds(row, 8), lo : lo + LANES] + acc[pl.ds(row + 256, 8), lo : lo + LANES]
            dep[x, z] = total * rows_to(wet_s[x, pl.ds(z, 1), :], 8)
        return carry

    lax.fori_loop(0, depth, finish_deposit, 0)

    for step, scale in enumerate((1.0 / 3.0, 0.5, 1.0)):
        if step > 0:
            for copy in halos(step):
                copy.start()
        for copy in halos(step):
            copy.wait_recv()

        def stage(z, carry, step=step, scale=scale):
            for x in range(width):

                def weight(d):
                    return rows_to(weights[d, x, pl.ds(z, 1), :], 8)

                centre = state[step, x + 1, z + 1]
                total = weight(0) * (state[step, x + 2, z + 1] - centre)
                total += weight(1) * (state[step, x, z + 1] - centre)
                total += weight(2) * (state[step, x + 1, z + 2] - centre)
                total += weight(3) * (state[step, x + 1, z] - centre)
                total += weight(4) * (pltpu.roll(centre, LANES - 1, 1) - centre)
                total += weight(5) * (pltpu.roll(centre, 1, 1) - centre)
                total -= dep[x, z] * centre
                new = state[0, x + 1, z + 1] + total * scale
                state[step + 1, x + 1, z + 1] = new
                if step == 2:
                    old_out[pl.ds(x * depth + z, tags, stride=width * depth), :] = new
                    carry = carry + new * rows_to(wet_s[x, pl.ds(z, 1), :] * emis[z], 8)
            return carry

        sums = lax.fori_loop(0, depth, stage, jnp.zeros((tags, LANES), F32))

    same_patch = (iota((LANES, LANES), 0) // 8 == iota((LANES, LANES), 1) // 8).astype(F32)
    patch = jnp.dot(sums, same_patch, precision=HIGHEST, preferred_element_type=F32)
    own_lane = iota((tags, LANES), 1) % 8 == iota((tags, LANES), 0)
    own_row = jnp.sum(jnp.where(own_lane, patch, 0.0), axis=0, keepdims=True)
    rows[0] = own_row

    def row_copy(j):
        return pltpu.make_async_remote_copy(
            src_ref=rows.at[0],
            dst_ref=rows.at[j],
            send_sem=s_row.at[j],
            recv_sem=r_row.at[j],
            device_id=(me, lax.rem(lev + j, n_lev)),
            device_id_type=MESH,
        )

    for j in range(1, n_lev):
        row_copy(j).start()

    def table(pair, carry):
        for x in range(width):
            values = jnp.concatenate(
                [state[3, x + 1, 2 * pair + 1], state[3, x + 1, 2 * pair + 2]], axis=0
            )
            first, second = split2(values)
            row = pl.multiple_of(((x & 1) * (depth // 2) + pair) * 16, 16)
            lo = (x >> 1) * LANES
            look[pl.ds(row, 16), lo : lo + LANES] = first
            look[pl.ds(row, 16), 256 + lo : 256 + lo + LANES] = second
        return carry

    lax.fori_loop(0, depth // 2, table, 0)
    total_row = own_row
    for j in range(1, n_lev):
        row_copy(j).wait_recv()
        total_row = total_row + rows[j]

    span_blocks = 4

    def read_group(g, carry):
        at = pl.ds(pl.multiple_of(g * span_blocks * LANES, span_blocks * LANES), span_blocks * LANES)
        hot = cell_b[:, at]
        found = jnp.dot(
            look[...], jnp.concatenate([hot, hot], axis=0), preferred_element_type=F32
        )
        for i in range(span_blocks):
            k = g * span_blocks + i
            hi_all = rows_to(cell_hi[pl.ds(k, 1), :], 8)
            value = jnp.zeros((8, LANES), F32)
            for hi in range(32):
                value += jnp.where(
                    hi_all == hi, found[hi * 8 : hi * 8 + 8, i * LANES : (i + 1) * LANES], 0.0
                )
            snd2[k, 0:tags, :] = value
            snd2[k, tags : tags + 1, :] = total_row

            @pl.when(k > 0)
            def _():
                back(k).start()

        return carry

    lax.fori_loop(0, n_tile // span_blocks, read_group, 0)
    rcv2[0] = snd2[0]

    for j in range(half // 2):
        for d in range(2):
            for i in range(2):
                if d * half + 2 * j + i > 0:
                    back(d * half + 2 * j + i).wait_recv()
            values = jnp.concatenate(
                [rcv2[d * half + 2 * j, 0:tags, :], rcv2[d * half + 2 * j + 1, 0:tags, :]], axis=0
            )
            first, second = split2(values)
            look2[16 * j : 16 * j + 16, d * LANES : (d + 1) * LANES] = first
            look2[16 * j : 16 * j + 16, 256 + d * LANES : 256 + (d + 1) * LANES] = second

    def sense_group(g, carry):
        at = pl.ds(pl.multiple_of(g * span_blocks * LANES, span_blocks * LANES), span_blocks * LANES)
        hot = pack_b[:, at]
        found = jnp.dot(
            look2[...], jnp.concatenate([hot, hot], axis=0), preferred_element_type=F32
        )
        for i in range(span_blocks):
            c = g * span_blocks + i
            one = pl.ds(pl.multiple_of(c * LANES, LANES), LANES)
            hi_all = rows_to(dest_hi[pl.ds(c, 1), :], 8)
            value = jnp.zeros((8, LANES), F32)
            for hi in range(half):
                value += jnp.where(
                    hi_all == hi, found[hi * 8 : hi * 8 + 8, i * LANES : (i + 1) * LANES], 0.0
                )
            sense_out[:, one] = value * coef[:, one]
        return carry

    lax.fori_loop(0, chunks // span_blocks, sense_group, 0)

    first_segment = ((me * n_lev + lev) * 8).astype(F32)
    wanted = iota((8, LANES), 0).astype(F32) + first_segment

    def add_tile(k, total):
        named = rows_to(rcv[lax.rem(n_tile - k, n_tile), tags + 1 : tags + 2, :], 8)
        values = rows_to(rcv2[k, tags : tags + 1, :], 8)
        return total + jnp.where(named == wanted, values, 0.0)

    by_segment = lax.fori_loop(0, n_tile, add_tile, jnp.zeros((8, LANES), F32))
    seg_out[...] = nt_dot(own_lane.astype(F32), by_segment, precision=HIGHEST)

    for copy in flows:
        copy.wait_send()
    for step in range(3):
        for copy in halos(step):
            copy.wait_send()
    for j in range(1, n_lev):
        row_copy(j).wait_send()

    def drain(k, carry):
        forward(k).wait_send()
        back(k).wait_send()
        return carry

    lax.fori_loop(1, n_tile, drain, 0)


def local(
    n_tile, n_lev, adjoint, courant, diffusion, heights, dep_coef, elem_dest, elem_cell, seg_map, emis_profile
):
    tags, width, depth, _ = adjoint.shape
    elements = dep_coef.shape[1]
    half = n_tile // 2
    vmem = pl.BlockSpec(memory_space=pltpu.VMEM)
    smem = pl.BlockSpec(memory_space=pltpu.SMEM)
    dma = pltpu.SemaphoreType.DMA
    group = min(8, n_tile)
    old, sense, segments = pl.pallas_call(
        functools.partial(step_kernel, n_tile, n_lev),
        out_shape=(
            jax.ShapeDtypeStruct((tags * width * depth, LANES), F32),
            jax.ShapeDtypeStruct((tags, elements), F32),
            jax.ShapeDtypeStruct((tags, 8), F32),
        ),
        in_specs=[vmem] * 8 + [smem],
        out_specs=(vmem, vmem, vmem),
        scratch_shapes=[
            pltpu.VMEM((4, width + 2, depth + 2, tags, LANES), F32),
            pltpu.VMEM((width, depth, tags, LANES), F32),
            pltpu.VMEM((6, width, depth, LANES), F32),
            pltpu.VMEM((width, depth, LANES), F32),
            pltpu.VMEM((2, 32, LANES), F32),
            pltpu.VMEM((2, 3, depth, LANES), F32),
            pltpu.VMEM((2, 2, depth, LANES), F32),
            pltpu.VMEM((2, 8, LANES), F32),
            pltpu.VMEM((2, 8, LANES), F32),
            pltpu.VMEM((elements // LANES * n_tile, LANES), BF16),
            pltpu.VMEM((elements // LANES * n_tile, 2 * LANES), F32),
            pltpu.VMEM((half * 18, elements), BF16),
            pltpu.VMEM((256, elements), BF16),
            pltpu.VMEM((n_tile, tags + 2, LANES), F32),
            pltpu.VMEM((n_tile, tags + 2, LANES), F32),
            pltpu.VMEM((512, group * LANES), BF16),
            pltpu.VMEM((256, n_tile * LANES), BF16),
            pltpu.VMEM((n_tile, LANES), I32),
            pltpu.VMEM((elements // LANES, LANES), I32),
            pltpu.VMEM((512, 256), F32),
            pltpu.VMEM((256, 512), BF16),
            pltpu.VMEM((n_tile, tags + 1, LANES), F32),
            pltpu.VMEM((n_tile, tags + 1, LANES), F32),
            pltpu.VMEM((half * 8, 512), BF16),
            pltpu.VMEM((n_lev, 1, LANES), F32),
            dma((n_tile,)),
            dma((n_tile,)),
            dma((n_tile,)),
            dma((n_tile,)),
            dma((4,)),
            dma((4,)),
            dma((3, 4)),
            dma((3, 4)),
            dma((n_lev,)),
            dma((n_lev,)),
        ],
        compiler_params=pltpu.CompilerParams(
            collective_id=0, has_side_effects=True, vmem_limit_bytes=56 << 20
        ),
        name="adjoint_step",
    )(
        adjoint.reshape(tags * width * depth, LANES),
        courant,
        diffusion,
        heights,
        dep_coef,
        elem_dest.reshape(elements // LANES, LANES),
        elem_cell.reshape(elements // LANES, LANES),
        seg_map,
        emis_profile,
    )
    return old.reshape(adjoint.shape), sense, segments


def solution(mesh):
    placed = (
        P(None, "tile", "lev", None),
        P(None, "tile", "lev", None),
        P("tile", "lev", None),
        P("tile", None),
        P(None, ("tile", "lev")),
        P(("tile", "lev"), None),
        P(("tile", "lev")),
        P("tile", None),
        P("lev"),
    )
    return jax.shard_map(
        functools.partial(local, mesh.shape["tile"], mesh.shape["lev"]),
        mesh=mesh,
        in_specs=placed,
        out_specs=(
            P(None, "tile", "lev", None),
            P(None, ("tile", "lev")),
            P(None, ("tile", "lev")),
        ),
        check_vma=False,
    )
```

time: 574 us -> 78.8 us (0.14)
  waiting for transfers between devices: 289 us -> 0 us
  local copies, waits for them, and re-layouts: 96.2 us -> 2.99 us
  starting transfers between devices: 91.3 us -> 0 us
  other arithmetic: 82.1 us -> 0 us
  Pallas kernels: 0 us -> 75 us
  between operations: 14.6 us -> 0.65 us
    unnamed x2 -> x0, waiting for transfers between devices: 281 us -> none
    pallas_call x0 -> x1, Pallas kernels: none -> 75 us  [local(): pl.pallas_call(functools.partial(step_kernel, n_tile, n_lev), out_shape=(...]
    scatter-add x2 -> x0, other arithmetic: 52.3 us -> none  [the longest x1 47 us: local(): jax.ops.segment_sum(arriving.T, safe_ids, num_segments=local_cells)]
    ppermute x16 -> x0, starting transfers between devices: 51.4 us -> none  [the longest x8 38.6 us: padded_2(): before = lax.ppermute(last, axis, up)]
    gather x3 -> x0, local copies, waits for them, and re-layouts: 48.9 us -> none  [the longest x2 32.7 us: local(): jnp.take(flat_old, safe_ids, axis=1) * arriving]
    all_to_all x2 -> x0, starting transfers between devices: 39.8 us -> none  [the longest x1 22.3 us: local(): lax.all_to_all(returning, 'tile', split_axis=1, concat_axis=1, tiled=True)]
    scatter x2 -> x0, local copies, waits for them, and re-layouts: 28.3 us -> none  [the longest x1 15.5 us: local(): cell_row = jnp.full((tile_count * CAP,), -1.0, jnp.float32).at[slot_index...]
    another operation x3 -> x0, other arithmetic: 19 us -> none
  transfers between devices with their start and end apart: 19 -> 0, of which waited for: 6 -> 0; matrix products, arithmetic and copies ran while one was open for 20% -> 0% of each run, Pallas kernels for 0% -> 0%
where the time goes in v1:
time: 78.8 us; the launch traced here: 78.6 us
  Pallas kernels  75 us (95%)
  local copies, waits for them, and re-layouts  2.99 us (4%)
    pallas_call x1, Pallas kernels, local(): pl.pallas_call(functools.partial(step_kernel, n_tile, n_lev), out_shape=(...  75 us
    unnamed x7, local copies, waits for them, and re-layouts  2.99 us

profile of v1, /device:TPU:1, one launch (start us, length us, event | category | flops | bytes accessed | tf_op | source)
XLA Modules:
  0.0 78.6 jit_solution(8588517870839321442)
XLA Ops:
  0.6 75.0 %adjoint_step.1 = (f32[512,128]{1,0:T(8,128)}, f32[8,4096]{1,0:T(8,128)}, f32[8,8]{1,0:T(8,128)}) custom-call(f32[512,128]{1,0:T(8,128)} %bitcast.4, f32[3,4,16,128]{3,2,1,0:T(8,128)} %cour.1, f32[4,16,128]{2,1,0:T(8,128)} %diff.1, s32[4,128]{1,0:T(4,128)} %hts.1, f32[8,4096]{1,0:T(8,128)} %coef.1, s32[32,128]{1,0:T(8,128)} %bitcast.6, s32[32,128]{1,0:T(8,128)} %bitcast.7, ...), custom_call_target="tpu_custom_call" | custom-call | tf_op jit(solution)/shard_map/adjoint_step/pallas_call | solution.py:537
  75.6 0.0 copy-start
  75.6 1.7 %copy.15 = f32[8,4,16,128]{3,2,1,0:T(8,128)} copy(f32[8,4,16,128]{3,2,1,0:T(8,128)} %bitcast.5) | data formatting | bytes 524288
  77.3 0.0 copy-done
  77.3 0.0 copy-start.1
  77.3 0.7 copy.16
  78.0 0.0 copy-done.1
  78.0 0.6 copy.17
Async XLA Ops:
  75.6 1.7 %copy-start = (f32[8,4096]{1,0:T(8,128)S(1)}, f32[8,4096]{1,0:T(8,128)}, u32[]{:S(2)}) copy-start(f32[8,4096]{1,0:T(8,128)} %get-tuple-element.13) | copy-start | bytes 393220
  77.3 0.7 copy-start.1

commit v2 on v1

--- a/solution.py
+++ b/solution.py
@@ -80,7 +80,7 @@
     snd2,
     rcv2,
     look2,
-    rows,
+    segs,
     s_a2a,
     r_a2a,
     s_back,
@@ -99,6 +99,7 @@
     tags, elements = coef.shape
     chunks = elements // LANES
     half = n_tile // 2
+    part = half // 2
     depth = 16
     width = 4
 
@@ -173,34 +174,22 @@
         zero = jnp.zeros((), BF16)
         for j in range(half // 2):
             chosen = local == jnp.full((), 2 * j, BF16)
-            pack_a[16 * j : 16 * j + 16, at] = jnp.where(chosen, first, zero)
-            pack_a[half * 8 + 16 * j : half * 8 + 16 * j + 16, at] = jnp.where(
-                chosen, second, zero
-            )
+            row = j // (part // 2) * part * 18 + j % (part // 2) * 16
+            pack_a[row : row + 16, at] = jnp.where(chosen, first, zero)
+            pack_a[row + part * 8 : row + part * 8 + 16, at] = jnp.where(chosen, second, zero)
         id_row = cell[pl.ds(c, 1), :].astype(F32)
         id_all = jnp.where(
             rows_to(hi_row, half) == iota((half, LANES), 0), rows_to(id_row, half), 0.0
         )
         id_first, id_second = split2(id_all)
-        pack_a[half * 16 : half * 17, at] = id_first
-        pack_a[half * 17 : half * 18, at] = id_second
+        for q in range(half // part):
+            row, own = q * part * 18 + part * 16, slice(q * part, q * part + part)
+            pack_a[row : row + part, at] = id_first[own]
+            pack_a[row + part : row + 2 * part, at] = id_second[own]
         return before + pref[block, LANES : 2 * LANES]
 
     lax.fori_loop(0, chunks, place, jnp.zeros((n_tile, LANES), F32))
-    packed = nt_dot(pack_a[...], pack_b[...])
-    for k in range(n_tile):
-        hi, lo = k % half, (k // half) * LANES
-        snd[k, 0:tags, :] = (
-            packed[hi * 8 : hi * 8 + 8, lo : lo + LANES]
-            + packed[half * 8 + hi * 8 : half * 8 + hi * 8 + 8, lo : lo + LANES]
-        )
-        snd[k, tags : tags + 1, :] = (
-            packed[half * 16 + hi : half * 16 + hi + 1, lo : lo + LANES]
-            + packed[half * 17 + hi : half * 17 + hi + 1, lo : lo + LANES]
-        )
-        snd[k, tags + 1 : tags + 2, :] = seg[0:1, :].astype(F32)
-
-    pl.semaphore_wait(barrier, n_tile - 1 + n_lev - 1)
+    seg_row = seg[0:1, :].astype(F32)
 
     def forward(k):
         return pltpu.make_async_remote_copy(
@@ -222,12 +211,26 @@
             device_id_type=MESH,
         )
 
-    def start_forward(k, carry):
-        forward(k).start()
-        return carry
-
-    lax.fori_loop(1, n_tile, start_forward, 0)
-    rcv[0] = snd[0]
+    for q in range(half // part):
+        packed = nt_dot(pack_a[q * part * 18 : (q + 1) * part * 18, :], pack_b[...])
+        if q == 0:
+            pl.semaphore_wait(barrier, n_tile - 1 + n_lev - 1)
+        for i in range(part):
+            for d in range(2):
+                k, lo = d * half + q * part + i, slice(d * LANES, (d + 1) * LANES)
+                at_id = part * 16 + i
+                snd[k, 0:tags, :] = (
+                    packed[i * 8 : i * 8 + 8, lo]
+                    + packed[part * 8 + i * 8 : part * 8 + i * 8 + 8, lo]
+                )
+                snd[k, tags : tags + 1, :] = (
+                    packed[at_id : at_id + 1, lo] + packed[at_id + part : at_id + part + 1, lo]
+                )
+                snd[k, tags + 1 : tags + 2, :] = seg_row
+                if k > 0:
+                    forward(k).start()
+                else:
+                    rcv[0] = snd[0]
 
     def halos(step):
         return [
@@ -370,55 +373,63 @@
 
     lax.fori_loop(0, depth, finish_deposit, 0)
 
-    for step, scale in enumerate((1.0 / 3.0, 0.5, 1.0)):
-        if step > 0:
-            for copy in halos(step):
-                copy.start()
-        for copy in halos(step):
-            copy.wait_recv()
-
-        def stage(z, carry, step=step, scale=scale):
-            for x in range(width):
-
-                def weight(d):
-                    return rows_to(weights[d, x, pl.ds(z, 1), :], 8)
-
-                centre = state[step, x + 1, z + 1]
-                total = weight(0) * (state[step, x + 2, z + 1] - centre)
-                total += weight(1) * (state[step, x, z + 1] - centre)
-                total += weight(2) * (state[step, x + 1, z + 2] - centre)
-                total += weight(3) * (state[step, x + 1, z] - centre)
-                total += weight(4) * (pltpu.roll(centre, LANES - 1, 1) - centre)
-                total += weight(5) * (pltpu.roll(centre, 1, 1) - centre)
-                total -= dep[x, z] * centre
-                new = state[0, x + 1, z + 1] + total * scale
-                state[step + 1, x + 1, z + 1] = new
-                if step == 2:
-                    old_out[pl.ds(x * depth + z, tags, stride=width * depth), :] = new
-                    carry = carry + new * rows_to(wet_s[x, pl.ds(z, 1), :] * emis[z], 8)
+    cells = [(x, z) for x in range(width) for z in range(depth)]
+    edge = [c for c in cells if c[0] in (0, width - 1) or c[1] in (0, depth - 1)]
+    inner = [c for c in cells if c not in edge]
+
+    def stage(step, which, sums):
+        for x, z in which:
+
+            def weight(d):
+                return rows_to(weights[d, x, z : z + 1, :], 8)
+
+            centre = state[step, x + 1, z + 1]
+            total = weight(0) * (state[step, x + 2, z + 1] - centre)
+            total += weight(1) * (state[step, x, z + 1] - centre)
+            total += weight(2) * (state[step, x + 1, z + 2] - centre)
+            total += weight(3) * (state[step, x + 1, z] - centre)
+            total += weight(4) * (pltpu.roll(centre, LANES - 1, 1) - centre)
+            total += weight(5) * (pltpu.roll(centre, 1, 1) - centre)
+            total -= dep[x, z] * centre
+            new = state[0, x + 1, z + 1] + total * (1.0 / 3.0, 0.5, 1.0)[step]
+            state[step + 1, x + 1, z + 1] = new
+            if step == 2:
+                old_out[pl.ds(x * depth + z, tags, stride=width * depth), :] = new
+                sums = sums + new * rows_to(wet_s[x, z : z + 1, :] * emis[z], 8)
+        return sums
+
+    def drain(copy):
+        def one(k, carry):
+            copy(k).wait_send()
             return carry
 
-        sums = lax.fori_loop(0, depth, stage, jnp.zeros((tags, LANES), F32))
+        lax.fori_loop(1, n_tile, one, 0)
+
+    sums = jnp.zeros((tags, LANES), F32)
+    for copy in halos(0):
+        copy.wait_recv()
+    stage(0, edge, sums)
+    for copy in halos(1):
+        copy.start()
+    stage(0, inner, sums)
+    stage(1, inner, sums)
+    drain(forward)
+    for copy in flows + halos(0):
+        copy.wait_send()
+    for copy in halos(1):
+        copy.wait_recv()
+    stage(1, edge, sums)
+    for copy in halos(2):
+        copy.start()
+    sums = stage(2, inner, sums)
+    for copy in halos(2):
+        copy.wait_recv()
+    sums = stage(2, edge, sums)
 
     same_patch = (iota((LANES, LANES), 0) // 8 == iota((LANES, LANES), 1) // 8).astype(F32)
     patch = jnp.dot(sums, same_patch, precision=HIGHEST, preferred_element_type=F32)
     own_lane = iota((tags, LANES), 1) % 8 == iota((tags, LANES), 0)
     own_row = jnp.sum(jnp.where(own_lane, patch, 0.0), axis=0, keepdims=True)
-    rows[0] = own_row
-
-    def row_copy(j):
-        return pltpu.make_async_remote_copy(
-            src_ref=rows.at[0],
-            dst_ref=rows.at[j],
-            send_sem=s_row.at[j],
-            recv_sem=r_row.at[j],
-            device_id=(me, lax.rem(lev + j, n_lev)),
-            device_id_type=MESH,
-        )
-
-    for j in range(1, n_lev):
-        row_copy(j).start()
-
     def table(pair, carry):
         for x in range(width):
             values = jnp.concatenate(
@@ -432,12 +443,7 @@
         return carry
 
     lax.fori_loop(0, depth // 2, table, 0)
-    total_row = own_row
-    for j in range(1, n_lev):
-        row_copy(j).wait_recv()
-        total_row = total_row + rows[j]
-
-    span_blocks = 4
+    span_blocks = min(8, chunks)
 
     def read_group(g, carry):
         at = pl.ds(pl.multiple_of(g * span_blocks * LANES, span_blocks * LANES), span_blocks * LANES)
@@ -454,7 +460,7 @@
                     hi_all == hi, found[hi * 8 : hi * 8 + 8, i * LANES : (i + 1) * LANES], 0.0
                 )
             snd2[k, 0:tags, :] = value
-            snd2[k, tags : tags + 1, :] = total_row
+            snd2[k, tags : tags + 1, :] = own_row
 
             @pl.when(k > 0)
             def _():
@@ -477,6 +483,37 @@
             look2[16 * j : 16 * j + 16, d * LANES : (d + 1) * LANES] = first
             look2[16 * j : 16 * j + 16, 256 + d * LANES : 256 + (d + 1) * LANES] = second
 
+    def wanted(j):
+        first_segment = (me * n_lev + lax.rem(lev + j, n_lev)) * 8
+        return (iota((8, LANES), 0) + first_segment).astype(F32)
+
+    def segment_copy(j):
+        return pltpu.make_async_remote_copy(
+            src_ref=segs.at[0, j],
+            dst_ref=segs.at[1, j],
+            send_sem=s_row.at[j],
+            recv_sem=r_row.at[j],
+            device_id=(me, lax.rem(lev + j, n_lev)),
+            device_id_type=MESH,
+        )
+
+    wanted_all = [wanted(j) for j in range(n_lev)]
+
+    def add_tile(k, totals):
+        named = rows_to(rcv[lax.rem(n_tile - k, n_tile), tags + 1 : tags + 2, :], 8)
+        values = rows_to(rcv2[k, tags : tags + 1, :], 8)
+        return tuple(
+            total + jnp.where(named == want, values, 0.0)
+            for total, want in zip(totals, wanted_all)
+        )
+
+    by_segment = lax.fori_loop(
+        0, n_tile, add_tile, (jnp.zeros((8, LANES), F32),) * n_lev, unroll=4
+    )
+    for j in range(1, n_lev):
+        segs[0, j] = by_segment[j]
+        segment_copy(j).start()
+
     def sense_group(g, carry):
         at = pl.ds(pl.multiple_of(g * span_blocks * LANES, span_blocks * LANES), span_blocks * LANES)
         hot = pack_b[:, at]
@@ -497,31 +534,15 @@
 
     lax.fori_loop(0, chunks // span_blocks, sense_group, 0)
 
-    first_segment = ((me * n_lev + lev) * 8).astype(F32)
-    wanted = iota((8, LANES), 0).astype(F32) + first_segment
-
-    def add_tile(k, total):
-        named = rows_to(rcv[lax.rem(n_tile - k, n_tile), tags + 1 : tags + 2, :], 8)
-        values = rows_to(rcv2[k, tags : tags + 1, :], 8)
-        return total + jnp.where(named == wanted, values, 0.0)
-
-    by_segment = lax.fori_loop(0, n_tile, add_tile, jnp.zeros((8, LANES), F32))
-    seg_out[...] = nt_dot(own_lane.astype(F32), by_segment, precision=HIGHEST)
-
-    for copy in flows:
+    drain(back)
+    for copy in halos(1) + halos(2):
         copy.wait_send()
-    for step in range(3):
-        for copy in halos(step):
-            copy.wait_send()
+
+    total = by_segment[0]
     for j in range(1, n_lev):
-        row_copy(j).wait_send()
-
-    def drain(k, carry):
-        forward(k).wait_send()
-        back(k).wait_send()
-        return carry
-
-    lax.fori_loop(1, n_tile, drain, 0)
+        segment_copy(j).wait()
+        total = total + segs[1, j]
+    seg_out[...] = nt_dot(own_lane.astype(F32), total, precision=HIGHEST)
 
 
 def local(
@@ -533,7 +554,7 @@
     vmem = pl.BlockSpec(memory_space=pltpu.VMEM)
     smem = pl.BlockSpec(memory_space=pltpu.SMEM)
     dma = pltpu.SemaphoreType.DMA
-    group = min(8, n_tile)
+    group = min(16, n_tile)
     old, sense, segments = pl.pallas_call(
         functools.partial(step_kernel, n_tile, n_lev),
         out_shape=(
@@ -568,7 +589,7 @@
             pltpu.VMEM((n_tile, tags + 1, LANES), F32),
             pltpu.VMEM((n_tile, tags + 1, LANES), F32),
             pltpu.VMEM((half * 8, 512), BF16),
-            pltpu.VMEM((n_lev, 1, LANES), F32),
+            pltpu.VMEM((2, n_lev, 8, LANES), F32),
             dma((n_tile,)),
             dma((n_tile,)),
             dma((n_tile,)),

time: 78.8 us -> 69.7 us (0.88)
  Pallas kernels: 75 us -> 65.9 us
    pallas_call x1, Pallas kernels: 75 us -> 65.9 us  [local(): pl.pallas_call(functools.partial(step_kernel, n_tile, n_lev), out_shape=(...]
where the time goes in v2:
time: 69.7 us; the launch traced here: 69.5 us
  Pallas kernels  65.9 us (95%)
  local copies, waits for them, and re-layouts  2.99 us (4%)
    pallas_call x1, Pallas kernels, local(): pl.pallas_call(functools.partial(step_kernel, n_tile, n_lev), out_shape=(...  65.9 us
    unnamed x7, local copies, waits for them, and re-layouts  2.99 us

profile of v2, /device:TPU:1, one launch (start us, length us, event | category | flops | bytes accessed | tf_op | source)
XLA Modules:
  0.0 69.5 jit_solution(14906901983308625100)
XLA Ops:
  0.6 65.9 %adjoint_step.1 = (f32[512,128]{1,0:T(8,128)}, f32[8,4096]{1,0:T(8,128)}, f32[8,8]{1,0:T(8,128)}) custom-call(f32[512,128]{1,0:T(8,128)} %bitcast.4, f32[3,4,16,128]{3,2,1,0:T(8,128)} %cour.1, f32[4,16,128]{2,1,0:T(8,128)} %diff.1, s32[4,128]{1,0:T(4,128)} %hts.1, f32[8,4096]{1,0:T(8,128)} %coef.1, s32[32,128]{1,0:T(8,128)} %bitcast.6, s32[32,128]{1,0:T(8,128)} %bitcast.7, ...), custom_call_target="tpu_custom_call" | custom-call | tf_op jit(solution)/shard_map/adjoint_step/pallas_call | solution.py:558
  66.5 0.0 copy-start
  66.5 1.7 %copy.15 = f32[8,4,16,128]{3,2,1,0:T(8,128)} copy(f32[8,4,16,128]{3,2,1,0:T(8,128)} %bitcast.5) | data formatting | bytes 524288
  68.2 0.0 copy-done
  68.2 0.0 copy-start.1
  68.2 0.7 copy.16
  68.9 0.0 copy-done.1
  68.9 0.6 copy.17
Async XLA Ops:
  66.5 1.7 %copy-start = (f32[8,4096]{1,0:T(8,128)S(1)}, f32[8,4096]{1,0:T(8,128)}, u32[]{:S(2)}) copy-start(f32[8,4096]{1,0:T(8,128)} %get-tuple-element.13) | copy-start | bytes 393220
  68.2 0.7 copy-start.1

commit v3 on v2

--- a/solution.py
+++ b/solution.py
@@ -91,6 +91,7 @@
     r_halo,
     s_row,
     r_row,
+    second_round,
 ):
     me = lax.axis_index("tile")
     lev = lax.axis_index("lev")
@@ -103,22 +104,20 @@
     depth = 16
     width = 4
 
+    count_z = min(8, n_tile)
+    count_y = n_tile // count_z
+    my_y, my_z = me // count_z, lax.rem(me, count_z)
     barrier = pltpu.get_barrier_semaphore()
 
-    def greet(k, carry):
-        pl.semaphore_signal(
-            barrier,
-            inc=1,
-            device_id=(lax.rem(me + k, n_tile), lev),
-            device_id_type=MESH,
-        )
-        return carry
-
-    lax.fori_loop(1, n_tile, greet, 0)
+    def signal(semaphore, tile, level):
+        pl.semaphore_signal(semaphore, inc=1, device_id=(tile, level), device_id_type=MESH)
+
+    for j in range(1, count_z):
+        signal(barrier, my_y * count_z + lax.rem(my_z + j, count_z), lev)
+    for j in range(1, count_y):
+        signal(barrier, lax.rem(my_y + j, count_y) * count_z + my_z, lev)
     for j in range(1, n_lev):
-        pl.semaphore_signal(
-            barrier, inc=1, device_id=(me, lax.rem(lev + j, n_lev)), device_id_type=MESH
-        )
+        signal(barrier, me, lax.rem(lev + j, n_lev))
 
     def reorder(z, carry):
         for x in range(width):
@@ -189,13 +188,17 @@
         return before + pref[block, LANES : 2 * LANES]
 
     lax.fori_loop(0, chunks, place, jnp.zeros((n_tile, LANES), F32))
+    pl.semaphore_wait(barrier, count_z - 1 + count_y - 1 + n_lev - 1)
+    for j in range(1, count_y):
+        signal(second_round, lax.rem(my_y + j, count_y) * count_z + my_z, lev)
+
     seg_row = seg[0:1, :].astype(F32)
 
     def forward(k):
         return pltpu.make_async_remote_copy(
             src_ref=snd.at[k],
             dst_ref=rcv.at[k],
-            send_sem=s_a2a.at[k],
+            send_sem=s_a2a,
             recv_sem=r_a2a.at[k],
             device_id=(lax.rem(me + k, n_tile), lev),
             device_id_type=MESH,
@@ -205,7 +208,7 @@
         return pltpu.make_async_remote_copy(
             src_ref=snd2.at[k],
             dst_ref=rcv2.at[k],
-            send_sem=s_back.at[k],
+            send_sem=s_back,
             recv_sem=r_back.at[k],
             device_id=(lax.rem(me + n_tile - k, n_tile), lev),
             device_id_type=MESH,
@@ -213,8 +216,8 @@
 
     for q in range(half // part):
         packed = nt_dot(pack_a[q * part * 18 : (q + 1) * part * 18, :], pack_b[...])
-        if q == 0:
-            pl.semaphore_wait(barrier, n_tile - 1 + n_lev - 1)
+        if q == 0 and count_y > 1:
+            pl.semaphore_wait(second_round, count_y - 1)
         for i in range(part):
             for d in range(2):
                 k, lo = d * half + q * part + i, slice(d * LANES, (d + 1) * LANES)
@@ -326,22 +329,27 @@
         weights[4, x] = ahead
         weights[5, x] = pltpu.roll(behind, 1, 1)
 
+    def slot(place_at):
+        source = lax.rem(place_at, count_y) * count_z + place_at // count_y
+        return lax.rem(me - source + n_tile, n_tile)
+
     group = dep_a.shape[1] // LANES
     acc[...] = jnp.zeros_like(acc)
 
     def gather_group(g, carry):
         for i in range(group):
-            k = g * group + i
+            place_at = g * group + i
+            k = slot(place_at)
 
             @pl.when(k > 0)
             def _():
                 forward(k).wait_recv()
 
-            at = pl.ds(pl.multiple_of(k * LANES, LANES), LANES)
+            at = pl.ds(pl.multiple_of(place_at * LANES, LANES), LANES)
             id_row = rcv[k, tags : tags + 1, :].astype(I32)
             hi_row = ((id_row >> 11) & 1) * 16 + ((id_row >> 7) & 15)
             lo_row = (id_row >> 12) * LANES + (id_row & 127)
-            cell_hi[pl.ds(k, 1), :] = hi_row
+            cell_hi[pl.ds(place_at, 1), :] = hi_row
             for j, piece in enumerate(one_hot_256(lo_row)):
                 cell_b[16 * j : 16 * j + 16, at] = piece
             first, second = split2(rcv[k, 0:tags, :])
@@ -398,12 +406,15 @@
                 sums = sums + new * rows_to(wet_s[x, z : z + 1, :] * emis[z], 8)
         return sums
 
-    def drain(copy):
-        def one(k, carry):
-            copy(k).wait_send()
-            return carry
-
-        lax.fori_loop(1, n_tile, one, 0)
+    def drain(source, target, semaphore):
+        pltpu.make_async_remote_copy(
+            src_ref=source.at[pl.ds(1, n_tile - 1)],
+            dst_ref=target.at[pl.ds(1, n_tile - 1)],
+            send_sem=semaphore,
+            recv_sem=semaphore,
+            device_id=(right, lev),
+            device_id_type=MESH,
+        ).wait_send()
 
     sums = jnp.zeros((tags, LANES), F32)
     for copy in halos(0):
@@ -413,7 +424,7 @@
         copy.start()
     stage(0, inner, sums)
     stage(1, inner, sums)
-    drain(forward)
+    drain(snd, rcv, s_a2a)
     for copy in flows + halos(0):
         copy.wait_send()
     for copy in halos(1):
@@ -452,8 +463,9 @@
             look[...], jnp.concatenate([hot, hot], axis=0), preferred_element_type=F32
         )
         for i in range(span_blocks):
-            k = g * span_blocks + i
-            hi_all = rows_to(cell_hi[pl.ds(k, 1), :], 8)
+            place_at = g * span_blocks + i
+            k = slot(place_at)
+            hi_all = rows_to(cell_hi[pl.ds(place_at, 1), :], 8)
             value = jnp.zeros((8, LANES), F32)
             for hi in range(32):
                 value += jnp.where(
@@ -471,17 +483,11 @@
     lax.fori_loop(0, n_tile // span_blocks, read_group, 0)
     rcv2[0] = snd2[0]
 
-    for j in range(half // 2):
-        for d in range(2):
-            for i in range(2):
-                if d * half + 2 * j + i > 0:
-                    back(d * half + 2 * j + i).wait_recv()
-            values = jnp.concatenate(
-                [rcv2[d * half + 2 * j, 0:tags, :], rcv2[d * half + 2 * j + 1, 0:tags, :]], axis=0
-            )
-            first, second = split2(values)
-            look2[16 * j : 16 * j + 16, d * LANES : (d + 1) * LANES] = first
-            look2[16 * j : 16 * j + 16, 256 + d * LANES : 256 + (d + 1) * LANES] = second
+    def arrive(k, carry):
+        back(k).wait_recv()
+        return carry
+
+    lax.fori_loop(1, n_tile, arrive, 0)
 
     def wanted(j):
         first_segment = (me * n_lev + lax.rem(lev + j, n_lev)) * 8
@@ -513,6 +519,15 @@
     for j in range(1, n_lev):
         segs[0, j] = by_segment[j]
         segment_copy(j).start()
+
+    for j in range(half // 2):
+        for d in range(2):
+            values = jnp.concatenate(
+                [rcv2[d * half + 2 * j, 0:tags, :], rcv2[d * half + 2 * j + 1, 0:tags, :]], axis=0
+            )
+            first, second = split2(values)
+            look2[16 * j : 16 * j + 16, d * LANES : (d + 1) * LANES] = first
+            look2[16 * j : 16 * j + 16, 256 + d * LANES : 256 + (d + 1) * LANES] = second
 
     def sense_group(g, carry):
         at = pl.ds(pl.multiple_of(g * span_blocks * LANES, span_blocks * LANES), span_blocks * LANES)
@@ -534,7 +549,7 @@
 
     lax.fori_loop(0, chunks // span_blocks, sense_group, 0)
 
-    drain(back)
+    drain(snd2, rcv2, s_back)
     for copy in halos(1) + halos(2):
         copy.wait_send()
 
@@ -590,9 +605,9 @@
             pltpu.VMEM((n_tile, tags + 1, LANES), F32),
             pltpu.VMEM((half * 8, 512), BF16),
             pltpu.VMEM((2, n_lev, 8, LANES), F32),
+            dma,
             dma((n_tile,)),
-            dma((n_tile,)),
-            dma((n_tile,)),
+            dma,
             dma((n_tile,)),
             dma((4,)),
             dma((4,)),
@@ -600,6 +615,7 @@
             dma((3, 4)),
             dma((n_lev,)),
             dma((n_lev,)),
+            pltpu.SemaphoreType.REGULAR,
         ],
         compiler_params=pltpu.CompilerParams(
             collective_id=0, has_side_effects=True, vmem_limit_bytes=56 << 20

time: 69.7 us -> 65.3 us (0.937)
  Pallas kernels: 65.9 us -> 61.5 us
    pallas_call x1, Pallas kernels: 65.9 us -> 61.5 us  [local(): pl.pallas_call(functools.partial(step_kernel, n_tile, n_lev), out_shape=(...]
where the time goes in v3:
time: 65.3 us; the launch traced here: 65.2 us
  Pallas kernels  61.5 us (94%)
  local copies, waits for them, and re-layouts  2.99 us (5%)
    pallas_call x1, Pallas kernels, local(): pl.pallas_call(functools.partial(step_kernel, n_tile, n_lev), out_shape=(...  61.5 us
    unnamed x7, local copies, waits for them, and re-layouts  2.99 us

profile of v3, /device:TPU:1, one launch (start us, length us, event | category | flops | bytes accessed | tf_op | source)
XLA Modules:
  0.0 65.2 jit_solution(14977138528067336763)
XLA Ops:
  0.6 61.5 %adjoint_step.1 = (f32[512,128]{1,0:T(8,128)}, f32[8,4096]{1,0:T(8,128)}, f32[8,8]{1,0:T(8,128)}) custom-call(f32[512,128]{1,0:T(8,128)} %bitcast.4, f32[3,4,16,128]{3,2,1,0:T(8,128)} %cour.1, f32[4,16,128]{2,1,0:T(8,128)} %diff.1, s32[4,128]{1,0:T(4,128)} %hts.1, f32[8,4096]{1,0:T(8,128)} %coef.1, s32[32,128]{1,0:T(8,128)} %bitcast.6, s32[32,128]{1,0:T(8,128)} %bitcast.7, ...), custom_call_target="tpu_custom_call" | custom-call | tf_op jit(solution)/shard_map/adjoint_step/pallas_call | solution.py:573
  62.2 0.0 copy-start
  62.2 1.7 %copy.15 = f32[8,4,16,128]{3,2,1,0:T(8,128)} copy(f32[8,4,16,128]{3,2,1,0:T(8,128)} %bitcast.5) | data formatting | bytes 524288
  63.9 0.0 copy-done
  63.9 0.0 copy-start.1
  63.9 0.7 %copy.16 = f32[8,4096]{1,0:T(8,128)} copy(f32[8,4096]{1,0:T(8,128)S(1)} %copy-done) | data formatting | bytes 262144
  64.5 0.0 copy-done.1
  64.6 0.6 copy.17
Async XLA Ops:
  62.2 1.7 %copy-start = (f32[8,4096]{1,0:T(8,128)S(1)}, f32[8,4096]{1,0:T(8,128)}, u32[]{:S(2)}) copy-start(f32[8,4096]{1,0:T(8,128)} %get-tuple-element.13) | copy-start | bytes 393220
  63.9 0.7 %copy-start.1 = (f32[8,8]{1,0:T(8,128)S(1)}, f32[8,8]{1,0:T(8,128)}, u32[]{:S(2)}) copy-start(f32[8,8]{1,0:T(8,128)} %get-tuple-element.14) | copy-start | bytes 772

commit v4 on v3

--- a/solution.py
+++ b/solution.py
@@ -39,6 +39,17 @@
     local = local.astype(F32).astype(BF16)
     one, zero = jnp.ones((), BF16), jnp.zeros((), BF16)
     return [jnp.where(local == jnp.full((), 16 * j, BF16), one, zero) for j in range(16)]
+
+
+EDGE_HI = 18
+HI_CELLS = (
+    [(0, z) for z in range(16)] + [(1, 0), (1, 15)] + [(1, z) for z in range(1, 15)]
+)
+
+
+def hi_lo(x, z):
+    middle = int(x in (1, 2))
+    return HI_CELLS.index((middle, z)), x // 2
 
 
 def step_kernel(
@@ -72,6 +83,7 @@
     snd,
     rcv,
     dep_a,
+    dep_i,
     cell_b,
     cell_hi,
     dest_hi,
@@ -100,7 +112,7 @@
     tags, elements = coef.shape
     chunks = elements // LANES
     half = n_tile // 2
-    part = half // 2
+    part = half
     depth = 16
     width = 4
 
@@ -118,27 +130,6 @@
         signal(barrier, lax.rem(my_y + j, count_y) * count_z + my_z, lev)
     for j in range(1, n_lev):
         signal(barrier, me, lax.rem(lev + j, n_lev))
-
-    def reorder(z, carry):
-        for x in range(width):
-            state[0, x + 1, z + 1] = adj[pl.ds(x * depth + z, tags, stride=width * depth), :]
-        return carry
-
-    lax.fori_loop(0, depth, reorder, 0)
-
-    levels = iota((depth, LANES), 0) + lev * depth
-    for x in range(width):
-        wet_s[x] = (levels >= rows_to(hts[x : x + 1, :], depth)).astype(F32)
-    fx_r[0, 0] = wet_s[width - 1]
-    fx_r[0, 1] = diff[width - 1]
-    fx_r[0, 2] = cour[0, width - 1]
-    fx_l[0, 0] = wet_s[0]
-    fx_l[0, 1] = diff[0]
-    for x in range(width):
-        fz_u[0, x : x + 1] = diff[x, depth - 1 : depth, :]
-        fz_u[0, width + x : width + x + 1] = cour[2, x, depth - 1 : depth, :]
-        fz_d[0, x : x + 1] = diff[x, 0:1, :]
-        fz_d[0, width + x : width + x + 1] = cour[2, x, 0:1, :]
 
     def mark(c, carry):
         k_row = (dest[pl.ds(c, 1), :] - me + n_tile) & (n_tile - 1)
@@ -234,6 +225,27 @@
                     forward(k).start()
                 else:
                     rcv[0] = snd[0]
+
+    def reorder(z, carry):
+        for x in range(width):
+            state[0, x + 1, z + 1] = adj[pl.ds(x * depth + z, tags, stride=width * depth), :]
+        return carry
+
+    lax.fori_loop(0, depth, reorder, 0)
+
+    levels = iota((depth, LANES), 0) + lev * depth
+    for x in range(width):
+        wet_s[x] = (levels >= rows_to(hts[x : x + 1, :], depth)).astype(F32)
+    fx_r[0, 0] = wet_s[width - 1]
+    fx_r[0, 1] = diff[width - 1]
+    fx_r[0, 2] = cour[0, width - 1]
+    fx_l[0, 0] = wet_s[0]
+    fx_l[0, 1] = diff[0]
+    for x in range(width):
+        fz_u[0, x : x + 1] = diff[x, depth - 1 : depth, :]
+        fz_u[0, width + x : width + x + 1] = cour[2, x, depth - 1 : depth, :]
+        fz_d[0, x : x + 1] = diff[x, 0:1, :]
+        fz_d[0, width + x : width + x + 1] = cour[2, x, 0:1, :]
 
     def halos(step):
         return [
@@ -334,6 +346,7 @@
         return lax.rem(me - source + n_tile, n_tile)
 
     group = dep_a.shape[1] // LANES
+    edge_rows, inner_rows = dep_a.shape[0] // 2, dep_i.shape[0] // 2
     acc[...] = jnp.zeros_like(acc)
 
     def gather_group(g, carry):
@@ -347,8 +360,11 @@
 
             at = pl.ds(pl.multiple_of(place_at * LANES, LANES), LANES)
             id_row = rcv[k, tags : tags + 1, :].astype(I32)
-            hi_row = ((id_row >> 11) & 1) * 16 + ((id_row >> 7) & 15)
-            lo_row = (id_row >> 12) * LANES + (id_row & 127)
+            z_row = (id_row >> 7) & 15
+            x_row = id_row >> 11
+            middle = jnp.where(z_row == 0, 16, jnp.where(z_row == 15, 17, z_row + 17))
+            hi_row = jnp.where((x_row == 1) | (x_row == 2), middle, z_row)
+            lo_row = (x_row >> 1) * LANES + (id_row & 127)
             cell_hi[pl.ds(place_at, 1), :] = hi_row
             for j, piece in enumerate(one_hot_256(lo_row)):
                 cell_b[16 * j : 16 * j + 16, at] = piece
@@ -357,33 +373,43 @@
             second = jnp.concatenate([second, second], axis=0)
             local = (rows_to(hi_row, 16) - sub_half).astype(F32).astype(BF16)
             zero = jnp.zeros((), BF16)
+            here = slice(i * LANES, (i + 1) * LANES)
             for j in range(16):
                 chosen = local == jnp.full((), 2 * j, BF16)
-                dep_a[16 * j : 16 * j + 16, i * LANES : (i + 1) * LANES] = jnp.where(
-                    chosen, first, zero
-                )
-                dep_a[256 + 16 * j : 272 + 16 * j, i * LANES : (i + 1) * LANES] = jnp.where(
-                    chosen, second, zero
-                )
+                first_j = jnp.where(chosen, first, zero)
+                second_j = jnp.where(chosen, second, zero)
+                if j < EDGE_HI // 2:
+                    dep_a[16 * j : 16 * j + 16, here] = first_j
+                    dep_a[edge_rows + 16 * j : edge_rows + 16 * j + 16, here] = second_j
+                else:
+                    row = 16 * j - edge_rows
+                    dep_i[row : row + 16, at] = first_j
+                    dep_i[inner_rows + row : inner_rows + row + 16, at] = second_j
         span = pl.ds(pl.multiple_of(g * group * LANES, group * LANES), group * LANES)
         acc[...] += nt_dot(dep_a[...], cell_b[:, span])
         return carry
 
     lax.fori_loop(0, n_tile // group, gather_group, 0)
 
-    def finish_deposit(z, carry):
-        for x in range(width):
-            row = pl.multiple_of(((x & 1) * depth + z) * 8, 8)
-            lo = (x >> 1) * LANES
-            total = acc[pl.ds(row, 8), lo : lo + LANES] + acc[pl.ds(row + 256, 8), lo : lo + LANES]
-            dep[x, z] = total * rows_to(wet_s[x, pl.ds(z, 1), :], 8)
-        return carry
-
-    lax.fori_loop(0, depth, finish_deposit, 0)
+    def deposit_of(which, total, rows):
+        for x, z in which:
+            hi, lo = hi_lo(x, z)
+            row, lo = hi * 8 % edge_rows, slice(lo * LANES, lo * LANES + LANES)
+            both = total[row : row + 8, lo] + total[row + rows : row + rows + 8, lo]
+            dep[x, z] = both * rows_to(wet_s[x, z : z + 1, :], 8)
+
+    def deposit_inner():
+        total = jnp.zeros((2 * inner_rows, 256), F32)
+        width_k = min(2048, n_tile * LANES)
+        for c in range(n_tile * LANES // width_k):
+            span = slice(c * width_k, (c + 1) * width_k)
+            total += nt_dot(dep_i[:, span], cell_b[:, span])
+        return total
 
     cells = [(x, z) for x in range(width) for z in range(depth)]
     edge = [c for c in cells if c[0] in (0, width - 1) or c[1] in (0, depth - 1)]
     inner = [c for c in cells if c not in edge]
+    deposit_of(edge, acc[...], edge_rows)
 
     def stage(step, which, sums):
         for x, z in which:
@@ -422,6 +448,7 @@
     stage(0, edge, sums)
     for copy in halos(1):
         copy.start()
+    deposit_of(inner, deposit_inner(), inner_rows)
     stage(0, inner, sums)
     stage(1, inner, sums)
     drain(snd, rcv, s_a2a)
@@ -441,19 +468,16 @@
     patch = jnp.dot(sums, same_patch, precision=HIGHEST, preferred_element_type=F32)
     own_lane = iota((tags, LANES), 1) % 8 == iota((tags, LANES), 0)
     own_row = jnp.sum(jnp.where(own_lane, patch, 0.0), axis=0, keepdims=True)
-    def table(pair, carry):
-        for x in range(width):
-            values = jnp.concatenate(
-                [state[3, x + 1, 2 * pair + 1], state[3, x + 1, 2 * pair + 2]], axis=0
-            )
-            first, second = split2(values)
-            row = pl.multiple_of(((x & 1) * (depth // 2) + pair) * 16, 16)
-            lo = (x >> 1) * LANES
-            look[pl.ds(row, 16), lo : lo + LANES] = first
-            look[pl.ds(row, 16), 256 + lo : 256 + lo + LANES] = second
-        return carry
-
-    lax.fori_loop(0, depth // 2, table, 0)
+    for pair in range(16):
+        for lo in range(2):
+            found = []
+            for middle, z in HI_CELLS[2 * pair : 2 * pair + 2]:
+                x = ((0, 3), (1, 2))[middle][lo]
+                found.append(state[3, x + 1, z + 1])
+            first, second = split2(jnp.concatenate(found, axis=0))
+            look[16 * pair : 16 * pair + 16, lo * LANES : (lo + 1) * LANES] = first
+            look[16 * pair : 16 * pair + 16, 256 + lo * LANES : 256 + (lo + 1) * LANES] = second
+
     span_blocks = min(8, chunks)
 
     def read_group(g, carry):
@@ -560,6 +584,27 @@
     seg_out[...] = nt_dot(own_lane.astype(F32), total, precision=HIGHEST)
 
 
+def write_kernel(old, sense, segments, old_out, sense_out, segments_out, sems):
+    pieces = 4
+    copies = []
+    for i in range(pieces):
+        for ref, out in ((old, old_out), (sense, sense_out)):
+            if ref is old:
+                rows = ref.shape[0] // pieces
+                at = (pl.ds(i * rows, rows),)
+            else:
+                lanes = ref.shape[1] // pieces
+                at = (slice(None), pl.ds(i * lanes, lanes))
+            copies.append(
+                pltpu.make_async_copy(ref.at[at], out.at[at], sems.at[len(copies)])
+            )
+    copies.append(pltpu.make_async_copy(segments, segments_out, sems.at[len(copies)]))
+    for copy in copies:
+        copy.start()
+    for copy in copies:
+        copy.wait()
+
+
 def local(
     n_tile, n_lev, adjoint, courant, diffusion, heights, dep_coef, elem_dest, elem_cell, seg_map, emis_profile
 ):
@@ -569,7 +614,7 @@
     vmem = pl.BlockSpec(memory_space=pltpu.VMEM)
     smem = pl.BlockSpec(memory_space=pltpu.SMEM)
     dma = pltpu.SemaphoreType.DMA
-    group = min(16, n_tile)
+    group = min(32, n_tile)
     old, sense, segments = pl.pallas_call(
         functools.partial(step_kernel, n_tile, n_lev),
         out_shape=(
@@ -595,11 +640,12 @@
             pltpu.VMEM((256, elements), BF16),
             pltpu.VMEM((n_tile, tags + 2, LANES), F32),
             pltpu.VMEM((n_tile, tags + 2, LANES), F32),
-            pltpu.VMEM((512, group * LANES), BF16),
+            pltpu.VMEM((16 * EDGE_HI, group * LANES), BF16),
+            pltpu.VMEM((512 - 16 * EDGE_HI, n_tile * LANES), BF16),
             pltpu.VMEM((256, n_tile * LANES), BF16),
             pltpu.VMEM((n_tile, LANES), I32),
             pltpu.VMEM((elements // LANES, LANES), I32),
-            pltpu.VMEM((512, 256), F32),
+            pltpu.VMEM((16 * EDGE_HI, 256), F32),
             pltpu.VMEM((256, 512), BF16),
             pltpu.VMEM((n_tile, tags + 1, LANES), F32),
             pltpu.VMEM((n_tile, tags + 1, LANES), F32),
@@ -632,6 +678,16 @@
         seg_map,
         emis_profile,
     )
+    anywhere = pl.BlockSpec(memory_space=pl.ANY)
+    results = (old, sense, segments)
+    old, sense, segments = pl.pallas_call(
+        write_kernel,
+        out_shape=tuple(jax.ShapeDtypeStruct(r.shape, r.dtype) for r in results),
+        in_specs=[vmem] * 3,
+        out_specs=(anywhere,) * 3,
+        scratch_shapes=[dma((9,))],
+        name="write_results",
+    )(*results)
     return old.reshape(adjoint.shape), sense, segments
 
 

time: 65.3 us -> 62.6 us (0.959)
  local copies, waits for them, and re-layouts: 2.99 us -> 0 us
    unnamed x7 -> x0, local copies, waits for them, and re-layouts: 2.99 us -> none
    pallas_call x0 -> x1, Pallas kernels: none -> 1.84 us  [local(): pl.pallas_call(write_kernel, out_shape=tuple((jax.ShapeDtypeStruct(r.shap...]
    pallas_call x1, Pallas kernels: 61.5 us -> 59.9 us  [local(): pl.pallas_call(functools.partial(step_kernel, n_tile, n_lev), out_shape=(...]
where the time goes in v4:
time: 62.6 us; the launch traced here: 62.4 us
  Pallas kernels  61.8 us (99%)
  between operations  0.64 us (1%)
    pallas_call x1, Pallas kernels, local(): pl.pallas_call(functools.partial(step_kernel, n_tile, n_lev), out_shape=(...  59.9 us
    pallas_call x1, Pallas kernels, local(): pl.pallas_call(write_kernel, out_shape=tuple((jax.ShapeDtypeStruct(r.shap...  1.84 us

profile of v4, /device:TPU:1, one launch (start us, length us, event | category | flops | bytes accessed | tf_op | source)
XLA Modules:
  0.0 62.4 jit_solution(16092857893703273098)
XLA Ops:
  0.6 59.9 %adjoint_step.1 = (f32[512,128]{1,0:T(8,128)}, f32[8,4096]{1,0:T(8,128)}, f32[8,8]{1,0:T(8,128)}) custom-call(f32[512,128]{1,0:T(8,128)} %bitcast.4, f32[3,4,16,128]{3,2,1,0:T(8,128)} %cour.1, f32[4,16,128]{2,1,0:T(8,128)} %diff.1, s32[4,128]{1,0:T(4,128)} %hts.1, f32[8,4096]{1,0:T(8,128)} %coef.1, s32[32,128]{1,0:T(8,128)} %bitcast.5, s32[32,128]{1,0:T(8,128)} %bitcast.6, ...), custom_call_target="tpu_custom_call" | custom-call | tf_op jit(solution)/shard_map/adjoint_step/pallas_call | solution.py:618
  60.6 1.8 %write_results.1 = (f32[512,128]{1,0:T(8,128)}, f32[8,4096]{1,0:T(8,128)}, f32[8,8]{1,0:T(8,128)}) custom-call(f32[512,128]{1,0:T(8,128)} %get-tuple-element.9.old, f32[8,4096]{1,0:T(8,128)} %get-tuple-element.10.sense, f32[8,8]{1,0:T(8,128)} %get-tuple-element.11.segments), custom_call_target="tpu_custom_call" | custom-call | tf_op jit(solution)/shard_map/write_results/pallas_call | solution.py:683

commit v5 on v4

--- a/solution.py
+++ b/solution.py
@@ -89,6 +89,7 @@
     dest_hi,
     acc,
     look,
+    inside,
     snd2,
     rcv2,
     look2,
@@ -460,6 +461,58 @@
     for copy in halos(2):
         copy.start()
     sums = stage(2, inner, sums)
+
+    def table(pairs):
+        for pair in pairs:
+            for lo in range(2):
+                found = []
+                for middle, z in HI_CELLS[2 * pair : 2 * pair + 2]:
+                    x = ((0, 3), (1, 2))[middle][lo]
+                    found.append(state[3, x + 1, z + 1])
+                first, second = split2(jnp.concatenate(found, axis=0))
+                at = slice(16 * pair, 16 * pair + 16)
+                look[at, lo * LANES : (lo + 1) * LANES] = first
+                look[at, 256 + lo * LANES : 256 + (lo + 1) * LANES] = second
+
+    span_blocks = min(8, chunks)
+    edge_hi, inner_hi = range(EDGE_HI), range(EDGE_HI, 32)
+
+    def read_span(numbers, final):
+        def read_group(g, carry):
+            at = pl.ds(
+                pl.multiple_of(g * span_blocks * LANES, span_blocks * LANES), span_blocks * LANES
+            )
+            hot = cell_b[:, at]
+            found = jnp.dot(
+                look[8 * numbers.start : 8 * numbers.stop, :],
+                jnp.concatenate([hot, hot], axis=0),
+                preferred_element_type=F32,
+            )
+            for i in range(span_blocks):
+                place_at = g * span_blocks + i
+                k = slot(place_at)
+                hi_all = rows_to(cell_hi[pl.ds(place_at, 1), :], 8)
+                value = inside[place_at] if final else jnp.zeros((8, LANES), F32)
+                for n, hi in enumerate(numbers):
+                    value += jnp.where(
+                        hi_all == hi, found[n * 8 : n * 8 + 8, i * LANES : (i + 1) * LANES], 0.0
+                    )
+                if not final:
+                    inside[place_at] = value
+                else:
+                    snd2[k, 0:tags, :] = value
+                    snd2[k, tags : tags + 1, :] = own_row
+
+                    @pl.when(k > 0)
+                    def _():
+                        back(k).start()
+
+            return carry
+
+        lax.fori_loop(0, n_tile // span_blocks, read_group, 0)
+
+    table(range(EDGE_HI // 2, 16))
+    read_span(inner_hi, False)
     for copy in halos(2):
         copy.wait_recv()
     sums = stage(2, edge, sums)
@@ -468,43 +521,8 @@
     patch = jnp.dot(sums, same_patch, precision=HIGHEST, preferred_element_type=F32)
     own_lane = iota((tags, LANES), 1) % 8 == iota((tags, LANES), 0)
     own_row = jnp.sum(jnp.where(own_lane, patch, 0.0), axis=0, keepdims=True)
-    for pair in range(16):
-        for lo in range(2):
-            found = []
-            for middle, z in HI_CELLS[2 * pair : 2 * pair + 2]:
-                x = ((0, 3), (1, 2))[middle][lo]
-                found.append(state[3, x + 1, z + 1])
-            first, second = split2(jnp.concatenate(found, axis=0))
-            look[16 * pair : 16 * pair + 16, lo * LANES : (lo + 1) * LANES] = first
-            look[16 * pair : 16 * pair + 16, 256 + lo * LANES : 256 + (lo + 1) * LANES] = second
-
-    span_blocks = min(8, chunks)
-
-    def read_group(g, carry):
-        at = pl.ds(pl.multiple_of(g * span_blocks * LANES, span_blocks * LANES), span_blocks * LANES)
-        hot = cell_b[:, at]
-        found = jnp.dot(
-            look[...], jnp.concatenate([hot, hot], axis=0), preferred_element_type=F32
-        )
-        for i in range(span_blocks):
-            place_at = g * span_blocks + i
-            k = slot(place_at)
-            hi_all = rows_to(cell_hi[pl.ds(place_at, 1), :], 8)
-            value = jnp.zeros((8, LANES), F32)
-            for hi in range(32):
-                value += jnp.where(
-                    hi_all == hi, found[hi * 8 : hi * 8 + 8, i * LANES : (i + 1) * LANES], 0.0
-                )
-            snd2[k, 0:tags, :] = value
-            snd2[k, tags : tags + 1, :] = own_row
-
-            @pl.when(k > 0)
-            def _():
-                back(k).start()
-
-        return carry
-
-    lax.fori_loop(0, n_tile // span_blocks, read_group, 0)
+    table(range(EDGE_HI // 2))
+    read_span(edge_hi, True)
     rcv2[0] = snd2[0]
 
     def arrive(k, carry):
@@ -585,7 +603,7 @@
 
 
 def write_kernel(old, sense, segments, old_out, sense_out, segments_out, sems):
-    pieces = 4
+    pieces = 1
     copies = []
     for i in range(pieces):
         for ref, out in ((old, old_out), (sense, sense_out)):
@@ -647,6 +665,7 @@
             pltpu.VMEM((elements // LANES, LANES), I32),
             pltpu.VMEM((16 * EDGE_HI, 256), F32),
             pltpu.VMEM((256, 512), BF16),
+            pltpu.VMEM((n_tile, tags, LANES), F32),
             pltpu.VMEM((n_tile, tags + 1, LANES), F32),
             pltpu.VMEM((n_tile, tags + 1, LANES), F32),
             pltpu.VMEM((half * 8, 512), BF16),

time: 62.6 us -> 62.4 us (level)
  no operation moved by 1% of the time
where the time goes in v5:
time: 62.4 us; the launch traced here: 62.3 us
  Pallas kernels  61.6 us (99%)
  between operations  0.64 us (1%)
    pallas_call x1, Pallas kernels, local(): pl.pallas_call(functools.partial(step_kernel, n_tile, n_lev), out_shape=(...  59.8 us
    pallas_call x1, Pallas kernels, local(): pl.pallas_call(write_kernel, out_shape=tuple((jax.ShapeDtypeStruct(r.shap...  1.85 us

profile of v5, /device:TPU:1, one launch (start us, length us, event | category | flops | bytes accessed | tf_op | source)
XLA Modules:
  0.0 62.3 jit_solution(1163082647921709513)
XLA Ops:
  0.6 59.8 %adjoint_step.1 = (f32[512,128]{1,0:T(8,128)}, f32[8,4096]{1,0:T(8,128)}, f32[8,8]{1,0:T(8,128)}) custom-call(f32[512,128]{1,0:T(8,128)} %bitcast.4, f32[3,4,16,128]{3,2,1,0:T(8,128)} %cour.1, f32[4,16,128]{2,1,0:T(8,128)} %diff.1, s32[4,128]{1,0:T(4,128)} %hts.1, f32[8,4096]{1,0:T(8,128)} %coef.1, s32[32,128]{1,0:T(8,128)} %bitcast.5, s32[32,128]{1,0:T(8,128)} %bitcast.6, ...), custom_call_target="tpu_custom_call" | custom-call | tf_op jit(solution)/shard_map/adjoint_step/pallas_call | solution.py:636
  60.4 1.8 %write_results.1 = (f32[512,128]{1,0:T(8,128)}, f32[8,4096]{1,0:T(8,128)}, f32[8,8]{1,0:T(8,128)}) custom-call(f32[512,128]{1,0:T(8,128)} %get-tuple-element.9.old, f32[8,4096]{1,0:T(8,128)} %get-tuple-element.10.sense, f32[8,8]{1,0:T(8,128)} %get-tuple-element.11.segments), custom_call_target="tpu_custom_call" | custom-call | tf_op jit(solution)/shard_map/write_results/pallas_call | solution.py:702
